TPU v7x, 128 devices: a whole 4x4x4 slice. The times are simulated.
128 devices in a mesh: lat: 8 (over y_hi, z), lon: 16 (over y_lo, x, core).
Axes of the slice: x: 4, y: 4 (y_hi: 2, y_lo: 2; y = y_hi * 2 + y_lo), z: 4, core: 2. Of those that a mesh axis runs over, the one named last changes fastest.
Arguments:
- satellite_blocks: bfloat16 [16384, 16, 128], P(('lat', 'lon')), may hold values from -6 to 6
- slot_source: int32 [128, 128, 4], P(('lat', 'lon')), may hold values from 0 to 127
- slot_weight: bfloat16 [128, 128, 4, 8, 128], P(('lat', 'lon')), may hold values from -2 to 2
- slot_target: int32 [128, 128, 4], P(('lat', 'lon')), may hold values from 0 to 63
- tile_counts: int32 [128, 128], P(('lat', 'lon')), may hold values from 0 to 4, as said below
- gate_input_weight: bfloat16 [128, 144], replicated, may hold values from -0.5 to 0.5
- gate_state_weight: bfloat16 [128, 288], replicated, may hold values from -0.375 to 0.375
- gate_bias: float32 [128], replicated, may hold values from -4 to 4
- hidden_init: bfloat16 [32, 256, 4096], P(None, 'lat', 'lon'), may hold values from -1 to 1
- cell_init: bfloat16 [32, 256, 4096], P(None, 'lat', 'lon'), may hold values from -6 to 6
Outputs:
- hidden_out: bfloat16 [32, 256, 4096], P(None, 'lat', 'lon')
- cell_out: bfloat16 [32, 256, 4096], P(None, 'lat', 'lon')
Inputs may be any that keep to these rules, and one draw needn't show every extreme that they name: slot_source[p, q, s] names one of the 128 blocks held by source device p. slot_target[q, p, s] is the cell block of tile q fed by slot s from device p. Only slots s < tile_counts[q, p] carry data from device p to tile q; at least one tile receives 4 blocks from every source device.
All inputs are finite; a program needn't handle non-finite values.
Results may differ from a plain program's by a relative error of at most 0.0069.
Values may be sent and summed in bfloat16 or wider, within the bound.
A program may use at most 128 MiB of HBM per device.

v0:
```python
import functools
import itertools
import random

import jax
import jax.numpy as jnp
import numpy as np
from jax import lax
from jax.experimental import pallas as pl
from jax.experimental.pallas import tpu as pltpu
from jax.sharding import PartitionSpec as P

STEPS = 3
MESH = pl.DeviceIdType.MESH
F32 = jnp.float32
BF16 = jnp.bfloat16
PEERS = 128
SLOTS = 4
CHUNKS = 4
ROWS = 32
COLS = 256
CH = 16
HID = 32


def send_order():
    offsets = [d for d in itertools.product(range(4), range(4), range(4), range(2)) if any(d)]
    random.Random(0).shuffle(offsets)
    return [(0, 0, 0, 0)] + offsets


ORDER = send_order()


def coords():
    i = lax.axis_index("lat")
    j = lax.axis_index("lon")
    return (lax.rem(lax.div(j, 2), 4), lax.div(i, 4) * 2 + lax.div(j, 8), lax.rem(i, 4), lax.rem(j, 2))


def device_at(x, y, z, c):
    return lax.div(y, 2) * 4 + z, lax.rem(y, 2) * 8 + x * 2 + c


def peer(offset):
    return device_at(*(lax.rem(a + d, m) for a, d, m in zip(coords(), offset, (4, 4, 4, 2))))


def peer_table(sign):
    table = np.array(ORDER, np.int32)
    at = [lax.rem(a + jnp.asarray((sign * table[:, k]) % m), m) for k, (a, m) in enumerate(zip(coords(), (4, 4, 4, 2)))]
    lat, lon = device_at(*at)
    return lat * 16 + lon


def lanes(shape):
    return lax.broadcasted_iota(jnp.int32, shape, len(shape) - 1)


def sublanes(shape):
    return lax.broadcasted_iota(jnp.int32, shape, len(shape) - 2)


def roll(x, shift):
    return pltpu.roll(x, shift, 1)


def band(n, to, to_index, ptab, stab, x_ref, w_ref):
    tile = ptab[n]
    lane = lanes((8, 128)) + sublanes((8, 128))
    inside = (lane >= 4) & (lane < 132)
    for s in range(SLOTS):
        x = x_ref[stab[tile * SLOTS + s]].astype(F32)
        w = jnp.where(inside, w_ref[tile, s].astype(F32), 0.0)
        total = w[4:5] * x
        for k in (0, 1, 2, 3, 5, 6, 7):
            total = total + w[k : k + 1] * roll(x, (4 - k) % 128)
        to[to_index, s] = total.astype(BF16)


def pick_columns(rows_ref, count, left_lane, right_lane):
    lane = lanes((count, 128))

    def one(y, total):
        row = pl.ds(pl.multiple_of(y * count, count), count)
        left = roll(rows_ref[0, row], lax.rem(y + 1 - left_lane + 128, 128))
        right = roll(rows_ref[1, row], lax.rem(y + 65 - right_lane + 128, 128))
        total = jnp.where(lane == y + 1, left, total)
        return jnp.where(lane == y + 65, right, total)

    return lax.fori_loop(0, ROWS, one, jnp.zeros((count, 128), F32), unroll=4)


def put_columns(rows_ref, count, columns):
    lane = lanes((count, 128))

    def one(y, carry):
        row = pl.ds(pl.multiple_of(y * count, count), count)
        left = roll(columns, lax.rem(127 - y, 128))
        right = roll(columns, lax.rem(190 - y, 128))
        rows_ref[0, row] = jnp.where(lane == 0, left, rows_ref[0, row])
        rows_ref[1, row] = jnp.where(lane == 127, right, rows_ref[1, row])
        return carry

    lax.fori_loop(0, ROWS, one, 0, unroll=4)


def spread(row, into, count, at):
    where = pl.ds(at, COLS)
    into[0:count, where] = roll(row, 1).astype(BF16)
    into[count : 2 * count, where] = row.astype(BF16)
    into[2 * count : 3 * count, where] = roll(row, COLS - 1).astype(BF16)


def row_at(rows_ref, y, count):
    row = pl.ds(pl.multiple_of(y * count, count), count)
    return jnp.concatenate([rows_ref[0, row], rows_ref[1, row]], axis=1)


def spread_rows(rows_ref, into, count):
    def one(y, carry):
        spread(row_at(rows_ref, y, count), into, count, pl.multiple_of((y + 1) * COLS, COLS))
        return carry

    lax.fori_loop(0, ROWS, one, 0, unroll=4)


def stage(rows_ref, count, edge, near, q_ref):
    last = (ROWS - 1) * count
    q_ref[0] = rows_ref[0, 0:count].astype(BF16)
    q_ref[1] = rows_ref[1, 0:count].astype(BF16)
    q_ref[2] = edge.astype(BF16)
    q_ref[3] = near.astype(BF16)
    q_ref[4] = rows_ref[0, last : last + count].astype(BF16)
    q_ref[5] = rows_ref[1, last : last + count].astype(BF16)


def swap(q_ref, r_ref, send_sem, recv_sem):
    i = lax.axis_index("lat")
    j = lax.axis_index("lon")
    up, down = lax.rem(i + 7, 8), lax.rem(i + 1, 8)
    left, right = lax.rem(j + 15, 16), lax.rem(j + 1, 16)
    plan = (
        ((up, j), 0, 4, 4),
        ((down, j), 2, 4, 0),
        ((i, left), 2, 1, 9),
        ((i, right), 2, 1, 8),
        ((up, left), 2, 1, 13),
        ((up, right), 2, 1, 12),
        ((down, left), 2, 1, 11),
        ((down, right), 2, 1, 10),
    )
    for target, source, size, slot in plan:
        pltpu.make_async_remote_copy(
            src_ref=q_ref.at[pl.ds(source, size)],
            dst_ref=r_ref.at[pl.ds(slot, size)],
            send_sem=send_sem,
            recv_sem=recv_sem,
            device_id=target,
            device_id_type=MESH,
        ).start()


def whole(r_ref, send_sem, recv_sem):
    i = lax.axis_index("lat")
    return pltpu.make_async_remote_copy(
        src_ref=r_ref,
        dst_ref=r_ref,
        send_sem=send_sem,
        recv_sem=recv_sem,
        device_id=(lax.rem(i + 1, 8), lax.axis_index("lon")),
        device_id_type=MESH,
    )


def edge_inputs(edge, near, r_ref, count):
    i = lax.axis_index("lat")
    lane = lanes((count, 128))
    half = lane < 64
    place = jnp.where(half, lane, lane - 64)
    top = (place == 0) & (i > 0)
    bottom = (place == 33) & (i < 7)
    middle = (place >= 1) & (place <= 32)
    got = lambda k: r_ref[k].astype(F32)

    def frame(mid, above, below):
        return jnp.where(middle, mid, jnp.where(top, above, jnp.where(bottom, below, 0.0)))

    edges = frame(edge, roll(got(0), 96), roll(got(6), 32))
    nears = frame(near, roll(got(1), 96), roll(got(7), 32))
    sides = frame(
        jnp.where(half, roll(got(8), 64), roll(got(9), 64)),
        jnp.where(half, roll(got(10), 32), roll(got(11), 32)),
        jnp.where(half, roll(got(12), 96), roll(got(13), 96)),
    )
    three = (jnp.where(half, sides, nears), edges, jnp.where(half, nears, sides))
    above = [roll(v, 1) for v in three]
    below = [roll(v, 127) for v in three]
    return jnp.concatenate([v.astype(BF16) for v in (*above, *three, *below)], axis=0)


def halo_rows(r_ref, into, count):
    i = lax.axis_index("lat")
    for slot, live, at in ((2, i > 0, 0), (4, i < 7, (ROWS + 1) * COLS)):
        row = jnp.concatenate([r_ref[slot].astype(F32), r_ref[slot + 1].astype(F32)], axis=1)
        spread(jnp.where(live, row, 0.0), into, count, at)


def update(gates, memory):
    ingate = jnp.tanh(gates[0:HID]) * 0.5 + 0.5
    forget = jnp.tanh(gates[HID : 2 * HID]) * 0.5 + 0.5
    outgate = jnp.tanh(gates[2 * HID : 3 * HID]) * 0.5 + 0.5
    memory = forget * memory + ingate * jnp.tanh(gates[3 * HID :])
    return outgate * jnp.tanh(memory), memory


def body(
    ptab, stab, x_ref, w_ref, aim_ref, from_ref, weight_ref, bias_ref, hid_ref, cell_ref,
    hout_ref, cout_ref,
    out_buf, in_buf, wide, sums, h0, h1, shifted, fc, fshifted, cells,
    qh, rh, qf, rf, far_send, far_recv, near_send, near_recv,
):
    barrier = pltpu.get_barrier_semaphore()
    for offset in ORDER[1:]:
        pl.semaphore_signal(barrier, inc=1, device_id=peer(offset), device_id_type=MESH)

    band(0, in_buf, 0, ptab, stab, x_ref, w_ref)

    def one_band(n, carry):
        band(n, out_buf, n, ptab, stab, x_ref, w_ref)
        return carry

    lax.fori_loop(1, PEERS, one_band, 0)

    for c in range(HID):
        for half in range(2):
            h0[half, pl.ds(c, ROWS, stride=HID), :] = hid_ref[c, :, half * 128 : half * 128 + 128].astype(F32)
    edge = pick_columns(h0, HID, 0, 127)
    near = pick_columns(h0, HID, 1, 126)
    stage(h0, HID, edge, near, qh.at[0])

    pl.semaphore_wait(barrier, PEERS - 1)
    swap(qh.at[0], rh.at[0], near_send.at[0], near_recv.at[0])
    size = PEERS // CHUNKS
    for n in range(1, PEERS):
        pltpu.make_async_remote_copy(
            src_ref=out_buf.at[n],
            dst_ref=in_buf.at[n],
            send_sem=far_send,
            recv_sem=far_recv.at[n // size],
            device_id=peer(ORDER[n]),
            device_id_type=MESH,
        ).start()

    for c in range(HID):
        for half in range(2):
            cells[half, pl.ds(c, ROWS, stride=HID), :] = cell_ref[c, :, half * 128 : half * 128 + 128].astype(F32)
    edge_cell = pick_columns(cells, HID, 0, 127)
    spread_rows(h0, shifted, HID)

    taken = size * SLOTS
    sums[...] = jnp.zeros_like(sums)
    for g in range(CHUNKS):
        first = 1 if g == 0 else g * size
        count = (g + 1) * size - first
        pltpu.make_async_remote_copy(
            src_ref=in_buf.at[pl.ds(first, count)],
            dst_ref=in_buf.at[pl.ds(first, count)],
            send_sem=far_send,
            recv_sem=far_recv.at[g],
            device_id=peer(ORDER[1]),
            device_id_type=MESH,
        ).wait_recv()

        def unpack(n, carry):
            block = in_buf[g * size + n].astype(F32).reshape(SLOTS * CH, 128)
            wide[pl.ds(pl.multiple_of(n * SLOTS * CH, SLOTS * CH), SLOTS * CH)] = block
            return carry

        lax.fori_loop(0, size, unpack, 0, unroll=4)
        spot = (sublanes((128, 128)) == from_ref[g : g + 1, :]).astype(F32).astype(BF16)
        aims = jnp.dot(aim_ref[...].astype(BF16), spot, preferred_element_type=F32)
        mine = sublanes((8, 128)) == lax.rem(lanes((8, 128)), SLOTS)
        aim = jnp.sum(jnp.where(mine, aims, 0.0), axis=0, keepdims=True)
        chosen = (sublanes((64, 128)).astype(F32) == aim).astype(F32).astype(BF16)
        for c in range(0, CH, 2):
            pair = [wide[pl.ds(c + k, taken, stride=CH), :].astype(BF16) for k in range(2)]
            part = jnp.dot(chosen, jnp.concatenate(pair, axis=1), preferred_element_type=F32)
            sums[c * 64 : c * 64 + 64] += part[:, :128]
            sums[c * 64 + 64 : c * 64 + 128] += part[:, 128:]

    def fill(y, carry):
        where = pl.ds(pl.multiple_of(y * CH, CH), CH)
        fc[0, where] = sums[pl.ds(2 * y, CH, stride=64), :]
        fc[1, where] = sums[pl.ds(2 * y + 1, CH, stride=64), :]
        return carry

    lax.fori_loop(0, ROWS, fill, 0, unroll=4)
    fedge = pick_columns(fc, CH, 0, 127)
    fnear = pick_columns(fc, CH, 1, 126)
    stage(fc, CH, fedge, fnear, qf)
    spread_rows(fc, fshifted, CH)
    swap(qf, rf, near_send.at[STEPS], near_recv.at[STEPS])

    bias = bias_ref[...]
    here, there = h0, h1
    fmini = None
    for t in range(STEPS):

        def one_row(y, carry):
            rhs = jnp.concatenate(
                [shifted[:, pl.ds(pl.multiple_of((y + a) * COLS, COLS), COLS)] for a in range(3)]
                + [fshifted[:, pl.ds(pl.multiple_of((y + a) * COLS, COLS), COLS)] for a in range(3)],
                axis=0,
            )
            gates = jnp.dot(weight_ref[...], rhs, preferred_element_type=F32) + bias
            where = pl.ds(pl.multiple_of(y * HID, HID), HID)
            hidden, memory = update(gates, row_at(cells, y, HID))
            for half in range(2):
                cells[half, where] = memory[:, half * 128 : half * 128 + 128]
                there[half, where] = hidden[:, half * 128 : half * 128 + 128]
            return carry

        lax.fori_loop(1, ROWS - 1, one_row, 0, unroll=2)

        whole(rh.at[t], near_send.at[t], near_recv.at[t]).wait_recv()
        if t == 0:
            whole(rf, near_send.at[STEPS], near_recv.at[STEPS]).wait_recv()
            fmini = edge_inputs(fedge, fnear, rf, CH)
            halo_rows(rf, fshifted, CH)
        mini = jnp.concatenate([edge_inputs(edge, near, rh.at[t], HID), fmini], axis=0)
        gates = jnp.dot(weight_ref[...], mini, preferred_element_type=F32) + bias[:, :128]
        edge, edge_cell = update(gates, edge_cell)
        halo_rows(rh.at[t], shifted, HID)
        one_row(0, 0)
        one_row(ROWS - 1, 0)
        put_columns(there, HID, edge)
        if t < STEPS - 1:
            near = pick_columns(there, HID, 1, 126)
            stage(there, HID, edge, near, qh.at[t + 1])
            spread_rows(there, shifted, HID)
            swap(qh.at[t + 1], rh.at[t + 1], near_send.at[t + 1], near_recv.at[t + 1])
        here, there = there, here

    put_columns(cells, HID, edge_cell)
    for c in range(HID):
        for half in range(2):
            part = slice(half * 128, half * 128 + 128)
            hout_ref[c, :, part] = here[half, pl.ds(c, ROWS, stride=HID), :].astype(BF16)
            cout_ref[c, :, part] = cells[half, pl.ds(c, ROWS, stride=HID), :].astype(BF16)

    pltpu.make_async_remote_copy(
        src_ref=in_buf.at[pl.ds(1, PEERS - 1)],
        dst_ref=in_buf.at[pl.ds(1, PEERS - 1)],
        send_sem=far_send,
        recv_sem=far_recv.at[0],
        device_id=peer(ORDER[1]),
        device_id_type=MESH,
    ).wait_send()
    for t in range(STEPS):
        whole(rh.at[t], near_send.at[t], near_recv.at[t]).wait_send()
    whole(rf, near_send.at[STEPS], near_recv.at[STEPS]).wait_send()


def on_device(
    satellite_blocks, slot_source, slot_weight, slot_target, tile_counts,
    gate_input_weight, gate_state_weight, gate_bias, hidden_init, cell_init,
):
    slot = jnp.arange(8, dtype=jnp.int32)[:, None]
    targets = jnp.pad(slot_target[0].T, ((0, 4), (0, 0)))
    aim = jnp.where(slot < tile_counts, targets, -1).astype(F32)
    sources = jnp.repeat(peer_table(-1).reshape(CHUNKS, -1), SLOTS, axis=1)
    scale = jnp.where(jnp.arange(128) < 96, 0.5, 1.0).astype(F32)
    weight = jnp.concatenate([gate_state_weight, gate_input_weight], axis=1)
    weight = weight * scale.astype(BF16)[:, None]
    bias = jnp.broadcast_to((gate_bias * scale)[:, None], (128, COLS))
    vmem = pl.BlockSpec(memory_space=pltpu.VMEM)
    smem = pl.BlockSpec(memory_space=pltpu.SMEM)
    wide_row = (3 * HID, (ROWS + 2) * COLS)
    return pl.pallas_call(
        body,
        out_shape=[jax.ShapeDtypeStruct((HID, ROWS, COLS), BF16)] * 2,
        in_specs=[smem, smem] + [vmem] * 8,
        out_specs=[vmem, vmem],
        scratch_shapes=[
            pltpu.VMEM((PEERS, SLOTS, CH, 128), BF16),
            pltpu.VMEM((PEERS, SLOTS, CH, 128), BF16),
            pltpu.VMEM((PEERS // CHUNKS * SLOTS * CH, 128), F32),
            pltpu.VMEM((CH * 64, 128), F32),
            pltpu.VMEM((2, ROWS * HID, 128), F32),
            pltpu.VMEM((2, ROWS * HID, 128), F32),
            pltpu.VMEM(wide_row, BF16),
            pltpu.VMEM((2, ROWS * CH, 128), F32),
            pltpu.VMEM((3 * CH, (ROWS + 2) * COLS), BF16),
            pltpu.VMEM((2, ROWS * HID, 128), F32),
            pltpu.VMEM((STEPS, 6, HID, 128), BF16),
            pltpu.VMEM((STEPS, 14, HID, 128), BF16),
            pltpu.VMEM((6, CH, 128), BF16),
            pltpu.VMEM((14, CH, 128), BF16),
            pltpu.SemaphoreType.DMA,
            pltpu.SemaphoreType.DMA((CHUNKS,)),
            pltpu.SemaphoreType.DMA((STEPS + 1,)),
            pltpu.SemaphoreType.DMA((STEPS + 1,)),
        ],
        compiler_params=pltpu.CompilerParams(
            collective_id=0, has_side_effects=True, vmem_limit_bytes=60 * 2**20
        ),
        name="reproject_and_step",
    )(
        peer_table(1), slot_source.reshape(-1), satellite_blocks, slot_weight[0], aim, sources,
        weight, bias, hidden_init, cell_init,
    )


def solution(mesh):
    placed = (
        P(("lat", "lon"), None, None),
        P(("lat", "lon"), None, None),
        P(("lat", "lon"), None, None, None, None),
        P(("lat", "lon"), None, None),
        P(("lat", "lon"), None),
        P(),
        P(),
        P(),
        P(None, "lat", "lon"),
        P(None, "lat", "lon"),
    )
    return jax.shard_map(
        on_device,
        mesh=mesh,
        in_specs=placed,
        out_specs=(P(None, "lat", "lon"), P(None, "lat", "lon")),
        check_vma=False,
    )
```

profile of v0, /device:TPU:1, one launch (start us, length us, event | category | flops | bytes accessed | tf_op | source)
XLA Modules:
  0.0 90.4 jit_solution(4556470802003582532)
XLA Ops:
  0.6 0.0 copy-start.9
  0.7 0.0 copy-start.10
  0.7 0.0 copy-start.11
  0.7 0.0 copy-start.12
  0.7 0.0 copy-start.6
  0.7 0.0 copy-start.7
  0.7 0.0 copy-start.8
  0.7 0.6 copy-done.9
  1.3 0.0 copy-done.10
  1.3 0.0 copy-done.11
  1.3 0.0 copy-done.12
  1.4 0.0 copy-done.6
  1.4 0.0 copy-done.7
  1.4 0.0 copy-done.8
  1.4 0.5 fusion.15
  1.9 0.7 copy-done.13
  2.6 0.0 copy-start.5
  2.6 0.1 reshape.21
  2.7 0.6 copy-done.4
  3.3 0.6 select_convert_fusion.aim_ref
  3.9 0.1 broadcast_in_dim.24
  4.0 0.7 reshape.22.from_ref
  4.7 0.1 copy.22
  4.8 0.7 reshape.20.stab
  5.5 0.1 copy.24
  5.6 0.1 copy-done.1
  5.7 0.1 copy.23
  5.8 0.8 maximum_multiply_fusion.weight_ref
  6.6 0.7 broadcast_in_dim.27.bias_ref
  7.3 80.3 %reproject_and_step.1 = (bf16[32,32,256]{2,1,0:T(8,128)(2,1)}, bf16[32,32,256]{2,1,0:T(8,128)(2,1)}) custom-call(s32[128]{0:T(128)} %get-tuple-element.3.ptab, s32[512]{0:T(512)} %reshape.20.stab, bf16[128,16,128]{2,1,0:T(8,128)(2,1)} %x_ref.1, bf16[128,4,8,128]{3,2,1,0:T(8,128)(2,1)} %bitcast.5, f32[8,128]{1,0:T(8,128)} %select_convert_fusion.aim_ref, ...), custom_call_target="tpu_custom_call" | custom-call | tf_op jit(solution)/shard_map/reproject_and_step/pallas_call | solution.py:380
  87.7 1.9 %copy.27 = bf16[32,32,256]{2,1,0:T(8,128)(2,1)} copy(bf16[32,32,256]{2,1,0:T(8,128)(2,1)} %get-tuple-element.6) | data formatting | bytes 1048576
  89.6 0.8 copy.28
  (12 shorter events, 0.0 us)
Async XLA Ops:
  0.6 0.7 copy-start.9
  0.7 0.7 copy-start.10
  0.7 0.7 copy-start.11
  0.7 0.7 copy-start.12
  0.7 0.7 copy-start.6
  0.7 0.7 copy-start.7
  0.7 0.7 copy-start.8
  1.9 0.7 copy-start.13
  2.6 0.7 copy-start.4
  2.6 0.7 copy-start.5
  3.9 0.7 copy-start.3
  4.7 0.8 copy-start.2
  4.8 0.9 copy-start.1
  87.6 1.9 %copy-start = (bf16[32,32,256]{2,1,0:T(8,128)(2,1)S(1)}, bf16[32,32,256]{2,1,0:T(8,128)(2,1)}, u32[]{:S(2)}) copy-start(bf16[32,32,256]{2,1,0:T(8,128)(2,1)} %get-tuple-element.7) | copy-start | bytes 1572868
where the time goes:
time: 90.7 us; the launch traced here: 90.4 us
  Pallas kernels  80.3 us (89%)
  local copies, waits for them, and re-layouts  7.36 us (8%)
  other arithmetic  1.9 us (2%)
    pallas_call x1, Pallas kernels, on_device(): pl.pallas_call(body, out_shape=[jax.ShapeDtypeStruct((HID, ROWS, COLS), B...  80.3 us
    unnamed x33, local copies, waits for them, and re-layouts  5.09 us

commit v1 on v0

v1 whole, which is shorter than its diff:
```python
import itertools
import random

import jax
import jax.numpy as jnp
import numpy as np
from jax import lax
from jax.experimental import pallas as pl
from jax.experimental.pallas import tpu as pltpu
from jax.sharding import PartitionSpec as P

STEPS = 3
MESH = pl.DeviceIdType.MESH
F32 = jnp.float32
BF16 = jnp.bfloat16
PEERS = 128
SLOTS = 4
SIZES = (64, 32, 16, 16)
STARTS = (0, 64, 96, 112)
GROUP = 8
BARRIER_AT = 16
UNROLL = 2
ROWS = 32
COLS = 256
CH = 16
HID = 32


def send_order():
    offsets = [d for d in itertools.product(range(4), range(4), range(4), range(2)) if any(d)]
    random.Random(0).shuffle(offsets)
    return [(0, 0, 0, 0)] + offsets


ORDER = send_order()


def coords():
    i = lax.axis_index("lat")
    j = lax.axis_index("lon")
    return (lax.rem(lax.div(j, 2), 4), lax.div(i, 4) * 2 + lax.div(j, 8), lax.rem(i, 4), lax.rem(j, 2))


def device_at(x, y, z, c):
    return lax.div(y, 2) * 4 + z, lax.rem(y, 2) * 8 + x * 2 + c


class Places:
    def __init__(self):
        x, y, z, c = coords()
        self.x = [lax.rem(x + d, 4) * 2 for d in range(4)]
        ys = [lax.rem(y + d, 4) for d in range(4)]
        self.y_lat = [lax.div(v, 2) * 4 for v in ys]
        self.y_lon = [lax.rem(v, 2) * 8 for v in ys]
        self.z = [lax.rem(z + d, 4) for d in range(4)]
        self.c = [lax.rem(c + d, 2) for d in range(2)]

    def __call__(self, offset, sign=1):
        dx, dy, dz, dc = ((sign * d) % m for d, m in zip(offset, (4, 4, 4, 2)))
        return self.y_lat[dy] + self.z[dz], self.y_lon[dy] + self.x[dx] + self.c[dc]

    def index(self, offset, sign=1):
        lat, lon = self(offset, sign)
        return lat * 16 + lon


def lanes(shape):
    return lax.broadcasted_iota(jnp.int32, shape, len(shape) - 1)


def sublanes(shape):
    return lax.broadcasted_iota(jnp.int32, shape, len(shape) - 2)


def roll(x, shift):
    return pltpu.roll(x, shift, 1)


def band(n, to, to_index, tab, stab, x_ref, w_ref):
    tile = tab[n]
    lane = lanes((8, 128)) + sublanes((8, 128))
    inside = (lane >= 4) & (lane < 132)
    for s in range(SLOTS):
        x = x_ref[stab[0, s, tile]].astype(F32)
        w = jnp.where(inside, w_ref[tile, s].astype(F32), 0.0)
        total = w[4:5] * x
        for k in (0, 1, 2, 3, 5, 6, 7):
            total = total + w[k : k + 1] * roll(x, (4 - k) % 128)
        to[to_index, s] = total.astype(BF16)


def row_at(rows_ref, y, count):
    row = pl.ds(pl.multiple_of(y * count, count), count)
    return rows_ref[0, row], rows_ref[1, row]


def spread(halves, into, count, at):
    row = jnp.concatenate(halves, axis=1)
    where = pl.ds(at, COLS)
    into[0:count, where] = roll(row, 1).astype(BF16)
    into[count : 2 * count, where] = row.astype(BF16)
    into[2 * count : 3 * count, where] = roll(row, COLS - 1).astype(BF16)


def padded_at(y):
    return (y + 1) * COLS if isinstance(y, int) else pl.multiple_of((y + 1) * COLS, COLS)


class Picker:
    def __init__(self, left_lane, right_lane, count):
        self.left, self.right = left_lane, right_lane
        self.shape = (count, 128)

    def empty(self):
        return jnp.zeros(self.shape, F32), jnp.zeros(self.shape, F32)

    def take(self, state, halves):
        lane = lanes(self.shape)
        return (
            jnp.where(lane == self.left, halves[0], roll(state[0], 1)),
            jnp.where(lane == self.right, halves[1], roll(state[1], 1)),
        )

    def place(self, state):
        lane = lanes(self.shape)
        left = roll(state[0], (1 - self.left) % 128)
        right = roll(state[1], (65 - self.right) % 128)
        return jnp.where((lane >= 1) & (lane <= 32), left, jnp.where((lane >= 65) & (lane <= 96), right, 0.0))


def corners(edge, y, halves):
    lane = lanes(edge.shape)
    left = roll(edge, (-(y + 1)) % 128)
    right = roll(edge, (62 - y) % 128)
    return jnp.where(lane == 0, left, halves[0]), jnp.where(lane == 127, right, halves[1])


def stage(q_ref, top, bottom, edge, near):
    for k, v in enumerate((top[0], top[1], edge, near, bottom[0], bottom[1])):
        q_ref[k] = v.astype(BF16)


def swap(q_ref, r_ref, send_sem, recv_sem):
    i = lax.axis_index("lat")
    j = lax.axis_index("lon")
    up, down = lax.rem(i + 7, 8), lax.rem(i + 1, 8)
    left, right = lax.rem(j + 15, 16), lax.rem(j + 1, 16)
    plan = (
        ((up, j), 0, 4, 4),
        ((down, j), 2, 4, 0),
        ((i, left), 2, 1, 9),
        ((i, right), 2, 1, 8),
        ((up, left), 2, 1, 13),
        ((up, right), 2, 1, 12),
        ((down, left), 2, 1, 11),
        ((down, right), 2, 1, 10),
    )
    for target, source, size, slot in plan:
        pltpu.make_async_remote_copy(
            src_ref=q_ref.at[pl.ds(source, size)],
            dst_ref=r_ref.at[pl.ds(slot, size)],
            send_sem=send_sem,
            recv_sem=recv_sem,
            device_id=target,
            device_id_type=MESH,
        ).start()


def whole(r_ref, send_sem, recv_sem):
    i = lax.axis_index("lat")
    return pltpu.make_async_remote_copy(
        src_ref=r_ref,
        dst_ref=r_ref,
        send_sem=send_sem,
        recv_sem=recv_sem,
        device_id=(lax.rem(i + 1, 8), lax.axis_index("lon")),
        device_id_type=MESH,
    )


def edge_inputs(edge, near, r_ref, count):
    i = lax.axis_index("lat")
    lane = lanes((count, 128))
    half = lane < 64
    place = jnp.where(half, lane, lane - 64)
    top = (place == 0) & (i > 0)
    bottom = (place == 33) & (i < 7)
    middle = (place >= 1) & (place <= 32)
    got = lambda k: r_ref[k].astype(F32)

    def frame(mid, above, below):
        return jnp.where(middle, mid, jnp.where(top, above, jnp.where(bottom, below, 0.0)))

    edges = frame(edge, roll(got(0), 96), roll(got(6), 32))
    nears = frame(near, roll(got(1), 96), roll(got(7), 32))
    sides = frame(
        jnp.where(half, roll(got(8), 64), roll(got(9), 64)),
        jnp.where(half, roll(got(10), 32), roll(got(11), 32)),
        jnp.where(half, roll(got(12), 96), roll(got(13), 96)),
    )
    three = (jnp.where(half, sides, nears), edges, jnp.where(half, nears, sides))
    above = [roll(v, 1) for v in three]
    below = [roll(v, 127) for v in three]
    return jnp.concatenate([v.astype(BF16) for v in (*above, *three, *below)], axis=0)


def halo_rows(r_ref, into, count):
    i = lax.axis_index("lat")
    for slot, live, at in ((2, i > 0, 0), (4, i < 7, (ROWS + 1) * COLS)):
        halves = [jnp.where(live, r_ref[slot + k].astype(F32), 0.0) for k in range(2)]
        spread(halves, into, count, at)


def update(gates, memory):
    ingate = jnp.tanh(gates[0:HID]) * 0.5 + 0.5
    forget = jnp.tanh(gates[HID : 2 * HID]) * 0.5 + 0.5
    outgate = jnp.tanh(gates[2 * HID : 3 * HID]) * 0.5 + 0.5
    memory = forget * memory + ingate * jnp.tanh(gates[3 * HID :])
    return outgate * jnp.tanh(memory), memory


def halves_of(v):
    return v[:, :128], v[:, 128:]


def body(
    stab, x_hbm, w_hbm, target_ref, count_ref, state_ref, input_ref, bias_ref, hid_hbm, cell_hbm,
    hout_ref, cout_ref,
    tab, x_ref, w_ref, hid_ref, cell_ref, weight, out_buf, in_buf, wide, sums, rows, s0, s1, fshifted, cells,
    qh, rh, qf, rf, load_sem, far_send, far_recv, near_send, near_recv,
):
    loads = [
        pltpu.make_async_copy(a, b, load_sem.at[k])
        for k, (a, b) in enumerate(((x_hbm, x_ref), (w_hbm, w_ref), (hid_hbm, hid_ref), (cell_hbm, cell_ref)))
    ]
    for copy in loads:
        copy.start()
    at = Places()
    barrier = pltpu.get_barrier_semaphore()
    tab[0] = at.index(ORDER[0])
    for n in range(1, PEERS):
        pl.semaphore_signal(barrier, inc=1, device_id=at(ORDER[n]), device_id_type=MESH)
        tab[n] = at.index(ORDER[n])
    loads[0].wait()
    loads[1].wait()

    def one_band(n, carry):
        band(n, out_buf, n, tab, stab, x_ref, w_ref)
        return carry

    def send(first, last):
        for n in range(max(first, 1), last):
            chunk = max(k for k in range(len(SIZES)) if STARTS[k] <= n)
            pltpu.make_async_remote_copy(
                src_ref=out_buf.at[n],
                dst_ref=in_buf.at[n],
                send_sem=far_send,
                recv_sem=far_recv.at[chunk],
                device_id=at(ORDER[n]),
                device_id_type=MESH,
            ).start()

    band(0, in_buf, 0, tab, stab, x_ref, w_ref)
    lax.fori_loop(1, GROUP, one_band, 0)
    for first in range(GROUP, PEERS, GROUP):
        lax.fori_loop(first, first + GROUP, one_band, 0)
        if first == BARRIER_AT:
            pl.semaphore_wait(barrier, PEERS - 1)
            send(0, first)
        elif first > BARRIER_AT:
            send(first - GROUP, first)
    send(PEERS - GROUP, PEERS)

    loads[2].wait()
    for c in range(HID):
        for half in range(2):
            rows[half, pl.ds(c, ROWS, stride=HID), :] = hid_ref[c, :, half * 128 : half * 128 + 128].astype(F32)
    outer, inner = Picker(0, 127, HID), Picker(1, 126, HID)

    def prepare(k, state):
        y = ROWS - 1 - k
        halves = row_at(rows, y, HID)
        spread(halves, s0, HID, padded_at(y))
        return outer.take(state[0], halves), inner.take(state[1], halves)

    state = lax.fori_loop(0, ROWS, prepare, (outer.empty(), inner.empty()), unroll=2)
    edge, near = outer.place(state[0]), inner.place(state[1])
    stage(qh.at[0], row_at(rows, 0, HID), row_at(rows, ROWS - 1, HID), edge, near)
    loads[3].wait()
    for c in range(HID):
        for half in range(2):
            cells[half, pl.ds(c, ROWS, stride=HID), :] = cell_ref[c, :, half * 128 : half * 128 + 128].astype(F32)
    swap(qh.at[0], rh.at[0], near_send.at[0], near_recv.at[0])

    def prepare_cell(k, state):
        return outer.take(state, row_at(cells, ROWS - 1 - k, HID))

    edge_cell = outer.place(lax.fori_loop(0, ROWS, prepare_cell, outer.empty(), unroll=2))

    scale = jnp.where(sublanes((128, 1)) < 3 * HID, 0.5, 1.0)
    bias = jnp.sum(jnp.where(sublanes((128, 128)) == lanes((128, 128)), bias_ref[...], 0.0), axis=1, keepdims=True)
    bias = bias * scale
    high = bias.astype(BF16).astype(F32)
    middle = (bias - high).astype(BF16).astype(F32)
    low = bias - high - middle
    lane = lanes((128, 128))
    extra = jnp.where(lane == 0, high, jnp.where(lane == 1, middle, jnp.where(lane == 2, low, 0.0)))
    taps = jnp.concatenate([state_ref[...].astype(F32), input_ref[...].astype(F32), extra.T[:80]], axis=0)
    deep = lax.broadcasted_iota(jnp.int32, (128, 128), 1)
    for k in range(4):
        part = taps[k * 128 : k * 128 + 128].T
        mult = jnp.where((deep + k * 128 < 432), scale, 1.0)
        weight[:, k * 128 : k * 128 + 128] = (part * mult).astype(BF16)
    ones = jnp.ones((16, COLS), BF16)

    counts = count_ref[...]
    aim4 = jnp.where(sublanes((SLOTS, 128)) < counts, target_ref[0], -1).astype(F32)
    aim8 = jnp.concatenate([aim4, aim4], axis=0).astype(BF16)
    sums[...] = jnp.zeros_like(sums)
    for g, (start, size) in enumerate(zip(STARTS, SIZES)):
        taken = size * SLOTS
        first = max(start, 1)
        got = in_buf.at[pl.ds(first, start + size - first)]
        pltpu.make_async_remote_copy(
            src_ref=got, dst_ref=got, send_sem=far_send, recv_sem=far_recv.at[g],
            device_id=at(ORDER[1]), device_id_type=MESH,
        ).wait_recv()

        def unpack(n, carry):
            block = in_buf[start + n].astype(F32).reshape(SLOTS * CH, 128)
            wide[pl.ds(pl.multiple_of(n * SLOTS * CH, SLOTS * CH), SLOTS * CH)] = block
            return carry

        lax.fori_loop(0, size, unpack, 0, unroll=4)
        which = lax.shift_right_logical(lanes((1, taken)), 2)
        origin = jnp.zeros((1, taken), jnp.int32)
        for n in range(size):
            origin = jnp.where(which == n, at.index(ORDER[start + n], -1), origin)
        spot = (sublanes((128, taken)) == origin).astype(F32).astype(BF16)
        aims = jnp.dot(aim8, spot, preferred_element_type=F32)
        mine = sublanes((8, taken)) == lanes((8, taken)) % SLOTS
        aim = jnp.sum(jnp.where(mine, aims, 0.0), axis=0, keepdims=True)
        chosen = (sublanes((64, taken)).astype(F32) == aim).astype(F32).astype(BF16)
        for c in range(0, CH, 2):
            pair = [wide[pl.ds(c + k, taken, stride=CH), :].astype(BF16) for k in range(2)]
            part = jnp.dot(chosen, jnp.concatenate(pair, axis=1), preferred_element_type=F32)
            sums[c * 64 : c * 64 + 64] += part[:, :128]
            sums[c * 64 + 64 : c * 64 + 128] += part[:, 128:]

    fouter, finner = Picker(0, 127, CH), Picker(1, 126, CH)

    def cell_row(y):
        return sums[pl.ds(2 * y, CH, stride=64), :], sums[pl.ds(2 * y + 1, CH, stride=64), :]

    def fill(k, state):
        y = ROWS - 1 - k
        halves = cell_row(y)
        spread(halves, fshifted, CH, padded_at(y))
        return fouter.take(state[0], halves), finner.take(state[1], halves)

    state = lax.fori_loop(0, ROWS, fill, (fouter.empty(), finner.empty()), unroll=2)
    fedge, fnear = fouter.place(state[0]), finner.place(state[1])
    stage(qf, cell_row(0), cell_row(ROWS - 1), fedge, fnear)
    swap(qf, rf, near_send.at[STEPS], near_recv.at[STEPS])

    fmini = None
    for t in range(STEPS):
        here, there = (s0, s1) if t % 2 == 0 else (s1, s0)
        last = t == STEPS - 1

        def one_row(y):
            spans = [pl.ds(padded_at(y - 1 + a), COLS) for a in range(3)]
            rhs = jnp.concatenate([here[:, w] for w in spans] + [fshifted[:, w] for w in spans] + [ones], axis=0)
            gates = jnp.dot(weight[:, :448], rhs, preferred_element_type=F32)
            hidden, memory = update(gates, jnp.concatenate(row_at(cells, y, HID), axis=1))
            halves = halves_of(hidden)
            where = pl.ds(pl.multiple_of(y * HID, HID), HID)
            for half, v in enumerate(halves_of(memory)):
                cells[half, where] = v
            if last:
                for half, v in enumerate(halves):
                    rows[half, where] = v
            else:
                spread(halves, there, HID, padded_at(y))
            return halves

        def inside(k, state):
            halves = one_row(ROWS - 2 - k)
            return state if last else inner.take(state, halves)

        state = lax.fori_loop(0, ROWS - 2, inside, 0 if last else inner.empty(), unroll=UNROLL)

        whole(rh.at[t], near_send.at[t], near_recv.at[t]).wait_recv()
        if t == 0:
            whole(rf, near_send.at[STEPS], near_recv.at[STEPS]).wait_recv()
            fmini = edge_inputs(fedge, fnear, rf, CH)
            halo_rows(rf, fshifted, CH)
        mini = jnp.concatenate([edge_inputs(edge, near, rh.at[t], HID), fmini, ones[:, :128]], axis=0)
        halo_rows(rh.at[t], here, HID)
        gates = jnp.dot(weight[:, :448], mini, preferred_element_type=F32)
        edge, edge_cell = update(gates, edge_cell)
        top = one_row(0)
        bottom = one_row(ROWS - 1)
        if last:
            break
        state = inner.take(state, top)
        far_left = roll(bottom[0], 31)
        far_right = roll(bottom[1], (96 - 126) % 128)
        spot = lanes((HID, 128))
        near = jnp.where(spot == 32, far_left, jnp.where(spot == 96, far_right, inner.place(state)))
        stage(qh.at[t + 1], corners(edge, 0, top), corners(edge, ROWS - 1, bottom), edge, near)
        swap(qh.at[t + 1], rh.at[t + 1], near_send.at[t + 1], near_recv.at[t + 1])

        def mend(y, state):
            v, u = state
            v_next, u_next = roll(v, 127), roll(u, 127)
            lane = lanes((HID, 128))
            first = pl.ds(padded_at(y), 128)
            second = pl.ds(pl.multiple_of((y + 1) * COLS + 128, 128), 128)
            for block, where, spot, value in (
                (0, first, 1, v), (1, first, 0, v_next), (1, second, 127, u), (2, second, 126, u_next),
            ):
                part = there.at[block * HID : block * HID + HID, where]
                part[...] = jnp.where(lane == spot, value, part[...].astype(F32)).astype(BF16)
            return v_next, u_next

        lax.fori_loop(0, ROWS, mend, (edge, roll(edge, 62)), unroll=4)

    def finish(y, state):
        v, u, vc, uc = state
        lane = lanes((HID, 128))
        for source, a, b, to in ((rows, v, u, hout_ref), (cells, vc, uc, cout_ref)):
            one, two = row_at(source, y, HID)
            to[y, :, :128] = jnp.where(lane == 0, a, one).astype(BF16)
            to[y, :, 128:] = jnp.where(lane == 127, b, two).astype(BF16)
        return tuple(roll(x, 127) for x in state)

    lax.fori_loop(
        0, ROWS, finish, (roll(edge, 127), roll(edge, 62), roll(edge_cell, 127), roll(edge_cell, 62)), unroll=4
    )

    sent = out_buf.at[pl.ds(1, PEERS - 1)]
    pltpu.make_async_remote_copy(
        src_ref=sent, dst_ref=sent, send_sem=far_send, recv_sem=far_recv.at[0],
        device_id=at(ORDER[1]), device_id_type=MESH,
    ).wait_send()
    for t in range(STEPS):
        whole(rh.at[t], near_send.at[t], near_recv.at[t]).wait_send()
    whole(rf, near_send.at[STEPS], near_recv.at[STEPS]).wait_send()


def on_device(
    satellite_blocks, slot_source, slot_weight, slot_target, tile_counts,
    gate_input_weight, gate_state_weight, gate_bias, hidden_init, cell_init,
):
    vmem = pl.BlockSpec(memory_space=pltpu.VMEM)
    smem = pl.BlockSpec(memory_space=pltpu.SMEM)
    hbm = pl.BlockSpec(memory_space=pl.ANY)
    padded = (ROWS + 2) * COLS
    hidden, memory = pl.pallas_call(
        body,
        out_shape=[jax.ShapeDtypeStruct((ROWS, HID, COLS), BF16)] * 2,
        in_specs=[smem, hbm, hbm] + [vmem] * 5 + [hbm, hbm],
        out_specs=[vmem, vmem],
        scratch_shapes=[
            pltpu.SMEM((PEERS,), jnp.int32),
            pltpu.VMEM((PEERS, CH, 128), BF16),
            pltpu.VMEM((PEERS, SLOTS, 8, 128), BF16),
            pltpu.VMEM((HID, ROWS, COLS), BF16),
            pltpu.VMEM((HID, ROWS, COLS), BF16),
            pltpu.VMEM((128, 512), BF16),
            pltpu.VMEM((PEERS, SLOTS, CH, 128), BF16),
            pltpu.VMEM((PEERS, SLOTS, CH, 128), BF16),
            pltpu.VMEM((max(SIZES) * SLOTS * CH, 128), F32),
            pltpu.VMEM((CH * 64, 128), F32),
            pltpu.VMEM((2, ROWS * HID, 128), F32),
            pltpu.VMEM((3 * HID, padded), BF16),
            pltpu.VMEM((3 * HID, padded), BF16),
            pltpu.VMEM((3 * CH, padded), BF16),
            pltpu.VMEM((2, ROWS * HID, 128), F32),
            pltpu.VMEM((STEPS, 6, HID, 128), BF16),
            pltpu.VMEM((STEPS, 14, HID, 128), BF16),
            pltpu.VMEM((6, CH, 128), BF16),
            pltpu.VMEM((14, CH, 128), BF16),
            pltpu.SemaphoreType.DMA((4,)),
            pltpu.SemaphoreType.DMA,
            pltpu.SemaphoreType.DMA((len(SIZES),)),
            pltpu.SemaphoreType.DMA((STEPS + 1,)),
            pltpu.SemaphoreType.DMA((STEPS + 1,)),
        ],
        compiler_params=pltpu.CompilerParams(
            collective_id=0, has_side_effects=True, vmem_limit_bytes=60 * 2**20
        ),
        name="reproject_and_step",
    )(
        slot_source.transpose(0, 2, 1), satellite_blocks, slot_weight[0], slot_target.transpose(0, 2, 1), tile_counts,
        gate_state_weight.T, gate_input_weight.T, gate_bias.reshape(1, -1), hidden_init, cell_init,
    )
    return hidden.transpose(1, 0, 2), memory.transpose(1, 0, 2)


def solution(mesh):
    placed = (
        P(("lat", "lon"), None, None),
        P(("lat", "lon"), None, None),
        P(("lat", "lon"), None, None, None, None),
        P(("lat", "lon"), None, None),
        P(("lat", "lon"), None),
        P(),
        P(),
        P(),
        P(None, "lat", "lon"),
        P(None, "lat", "lon"),
    )
    return jax.shard_map(
        on_device,
        mesh=mesh,
        in_specs=placed,
        out_specs=(P(None, "lat", "lon"), P(None, "lat", "lon")),
        check_vma=False,
    )
```

time: 90.7 us -> 69.4 us (0.77)
  Pallas kernels: 80.3 us -> 65.3 us
  local copies, waits for them, and re-layouts: 7.36 us -> 3.27 us
  other arithmetic: 1.9 us -> 0 us
    pallas_call x1, Pallas kernels: 80.3 us -> 65.3 us  [on_device(): pl.pallas_call(body, out_shape=[jax.ShapeDtypeStruct((ROWS, HID, COLS), B...]
    unnamed x33 -> x4, local copies, waits for them, and re-layouts: 5.09 us -> 3.27 us
    reshape x3 -> x0, local copies, waits for them, and re-layouts: 1.47 us -> none  [the longest x2 0.78 us: on_device(): sources = jnp.repeat(peer_table(-1).reshape(CHUNKS, -1), SLOTS, axis=1)]
where the time goes in v1:
time: 69.4 us; the launch traced here: 69.2 us
  Pallas kernels  65.3 us (94%)
  local copies, waits for them, and re-layouts  3.27 us (5%)
    pallas_call x1, Pallas kernels, on_device(): pl.pallas_call(body, out_shape=[jax.ShapeDtypeStruct((ROWS, HID, COLS), B...  65.3 us
    unnamed x4, local copies, waits for them, and re-layouts  3.27 us

profile of v1, /device:TPU:1, one launch (start us, length us, event | category | flops | bytes accessed | tf_op | source)
XLA Modules:
  0.0 69.2 jit_solution(13994612047514994099)
XLA Ops:
  0.6 65.3 %reproject_and_step.1 = (bf16[32,32,256]{2,1,0:T(8,128)(2,1)}, bf16[32,32,256]{2,1,0:T(8,128)(2,1)}) custom-call(s32[1,4,128]{2,1,0:T(4,128)} %bitcast.13, bf16[128,16,128]{2,1,0:T(8,128)(2,1)} %x_hbm.1, bf16[128,4,8,128]{3,2,1,0:T(8,128)(2,1)} %bitcast.8, s32[1,4,128]{2,1,0:T(4,128)} %bitcast.14, s32[1,128]{1,0:T(1,128)} %count_ref.1, ...), custom_call_target="tpu_custom_call" | custom-call | tf_op jit(solution)/shard_map/reproject_and_step/pallas_call | solution.py:460
  66.0 0.0 copy-start
  66.0 2.2 %copy.12 = bf16[32,32,256]{2,1,0:T(8,128)(2,1)} copy(bf16[32,32,256]{2,0,1:T(8,128)(2,1)} %bitcast.10) | data formatting | bytes 1048576
  68.1 0.0 copy-done
  68.2 1.1 %copy.13 = bf16[32,32,256]{2,1,0:T(8,128)(2,1)} copy(bf16[32,32,256]{2,0,1:T(8,128)(2,1)S(1)} %bitcast.9) | data formatting | bytes 1048576
Async XLA Ops:
  66.0 2.2 %copy-start = (bf16[32,32,256]{2,1,0:T(8,128)(2,1)S(1)}, bf16[32,32,256]{2,1,0:T(8,128)(2,1)}, u32[]{:S(2)}) copy-start(bf16[32,32,256]{2,1,0:T(8,128)(2,1)} %get-tuple-element.5) | copy-start | bytes 1572868

commit v2 on v1

--- a/solution.py
+++ b/solution.py
@@ -19,7 +19,7 @@
 STARTS = (0, 64, 96, 112)
 GROUP = 8
 BARRIER_AT = 16
-UNROLL = 2
+BLOCK = 5
 ROWS = 32
 COLS = 256
 CH = 16
@@ -226,7 +226,7 @@
 def body(
     stab, x_hbm, w_hbm, target_ref, count_ref, state_ref, input_ref, bias_ref, hid_hbm, cell_hbm,
     hout_ref, cout_ref,
-    tab, x_ref, w_ref, hid_ref, cell_ref, weight, out_buf, in_buf, wide, sums, rows, s0, s1, fshifted, cells,
+    tab, x_ref, w_ref, hid_ref, cell_ref, weight, out_buf, in_buf, wide, sums, rows, s0, s1, fshifted, cells, ga, gb,
     qh, rh, qf, rf, load_sem, far_send, far_recv, near_send, near_recv,
 ):
     loads = [
@@ -238,8 +238,9 @@
     at = Places()
     barrier = pltpu.get_barrier_semaphore()
     tab[0] = at.index(ORDER[0])
+    for offset in sorted(ORDER[1:], key=lambda d: -sum(min(a, 4 - a) for a in d[:3])):
+        pl.semaphore_signal(barrier, inc=1, device_id=at(offset), device_id_type=MESH)
     for n in range(1, PEERS):
-        pl.semaphore_signal(barrier, inc=1, device_id=at(ORDER[n]), device_id_type=MESH)
         tab[n] = at.index(ORDER[n])
     loads[0].wait()
     loads[1].wait()
@@ -347,19 +348,18 @@
             sums[c * 64 : c * 64 + 64] += part[:, :128]
             sums[c * 64 + 64 : c * 64 + 128] += part[:, 128:]
 
-    fouter, finner = Picker(0, 127, CH), Picker(1, 126, CH)
-
     def cell_row(y):
         return sums[pl.ds(2 * y, CH, stride=64), :], sums[pl.ds(2 * y + 1, CH, stride=64), :]
 
-    def fill(k, state):
-        y = ROWS - 1 - k
+    spot = lanes((CH, 128))
+    fedge = fnear = jnp.zeros((CH, 128), F32)
+    for y in range(ROWS):
         halves = cell_row(y)
         spread(halves, fshifted, CH, padded_at(y))
-        return fouter.take(state[0], halves), finner.take(state[1], halves)
-
-    state = lax.fori_loop(0, ROWS, fill, (fouter.empty(), finner.empty()), unroll=2)
-    fedge, fnear = fouter.place(state[0]), finner.place(state[1])
+        fedge = jnp.where(spot == y + 1, roll(halves[0], y + 1), fedge)
+        fedge = jnp.where(spot == y + 65, roll(halves[1], (y + 66) % 128), fedge)
+        fnear = jnp.where(spot == y + 1, roll(halves[0], y), fnear)
+        fnear = jnp.where(spot == y + 65, roll(halves[1], (y + 67) % 128), fnear)
     stage(qf, cell_row(0), cell_row(ROWS - 1), fedge, fnear)
     swap(qf, rf, near_send.at[STEPS], near_recv.at[STEPS])
 
@@ -368,10 +368,13 @@
         here, there = (s0, s1) if t % 2 == 0 else (s1, s0)
         last = t == STEPS - 1
 
-        def one_row(y):
-            spans = [pl.ds(padded_at(y - 1 + a), COLS) for a in range(3)]
-            rhs = jnp.concatenate([here[:, w] for w in spans] + [fshifted[:, w] for w in spans] + [ones], axis=0)
-            gates = jnp.dot(weight[:, :448], rhs, preferred_element_type=F32)
+        def gates_of(y, count=1):
+            spans = [pl.ds(padded_at(y - 1 + a), COLS * count) for a in range(3)]
+            fixed = jnp.ones((16, COLS * count), BF16)
+            rhs = jnp.concatenate([here[:, w] for w in spans] + [fshifted[:, w] for w in spans] + [fixed], axis=0)
+            return jnp.dot(weight[:, :448], rhs, preferred_element_type=F32)
+
+        def finish_row(y, gates):
             hidden, memory = update(gates, jnp.concatenate(row_at(cells, y, HID), axis=1))
             halves = halves_of(hidden)
             where = pl.ds(pl.multiple_of(y * HID, HID), HID)
@@ -384,11 +387,22 @@
                 spread(halves, there, HID, padded_at(y))
             return halves
 
+        def block(low, buffer, state):
+            for r in range(BLOCK - 1, -1, -1):
+                halves = finish_row(low + r, buffer[:, r * COLS : r * COLS + COLS])
+                state = state if last else inner.take(state, halves)
+            return state
+
         def inside(k, state):
-            halves = one_row(ROWS - 2 - k)
-            return state if last else inner.take(state, halves)
-
-        state = lax.fori_loop(0, ROWS - 2, inside, 0 if last else inner.empty(), unroll=UNROLL)
+            low = ROWS - 1 - BLOCK - 2 * BLOCK * k
+            gb[...] = gates_of(low - BLOCK, BLOCK)
+            state = block(low, ga, state)
+            ga[...] = gates_of(lax.max(low - 2 * BLOCK, 1), BLOCK)
+            return block(low - BLOCK, gb, state)
+
+        ga[...] = gates_of(ROWS - 1 - BLOCK, BLOCK)
+        state = 0 if last else inner.empty()
+        state = lax.fori_loop(0, (ROWS - 2) // (2 * BLOCK), inside, state)
 
         whole(rh.at[t], near_send.at[t], near_recv.at[t]).wait_recv()
         if t == 0:
@@ -399,8 +413,9 @@
         halo_rows(rh.at[t], here, HID)
         gates = jnp.dot(weight[:, :448], mini, preferred_element_type=F32)
         edge, edge_cell = update(gates, edge_cell)
-        top = one_row(0)
-        bottom = one_row(ROWS - 1)
+        tops, bottoms = gates_of(0), gates_of(ROWS - 1)
+        top = finish_row(0, tops)
+        bottom = finish_row(ROWS - 1, bottoms)
         if last:
             break
         state = inner.take(state, top)
@@ -411,33 +426,24 @@
         stage(qh.at[t + 1], corners(edge, 0, top), corners(edge, ROWS - 1, bottom), edge, near)
         swap(qh.at[t + 1], rh.at[t + 1], near_send.at[t + 1], near_recv.at[t + 1])
 
-        def mend(y, state):
-            v, u = state
-            v_next, u_next = roll(v, 127), roll(u, 127)
-            lane = lanes((HID, 128))
-            first = pl.ds(padded_at(y), 128)
-            second = pl.ds(pl.multiple_of((y + 1) * COLS + 128, 128), 128)
-            for block, where, spot, value in (
-                (0, first, 1, v), (1, first, 0, v_next), (1, second, 127, u), (2, second, 126, u_next),
+        lane = lanes((HID, 128))
+        left = [roll(edge, -y % 128).astype(BF16) for y in range(ROWS + 1)]
+        right = [roll(edge, (62 - y) % 128).astype(BF16) for y in range(ROWS + 1)]
+        for y in range(ROWS):
+            first = pl.ds((y + 1) * COLS, 128)
+            second = pl.ds((y + 1) * COLS + 128, 128)
+            for block_at, where, spot, value in (
+                (0, first, 1, left[y]), (1, first, 0, left[y + 1]),
+                (1, second, 127, right[y]), (2, second, 126, right[y + 1]),
             ):
-                part = there.at[block * HID : block * HID + HID, where]
-                part[...] = jnp.where(lane == spot, value, part[...].astype(F32)).astype(BF16)
-            return v_next, u_next
-
-        lax.fori_loop(0, ROWS, mend, (edge, roll(edge, 62)), unroll=4)
-
-    def finish(y, state):
-        v, u, vc, uc = state
-        lane = lanes((HID, 128))
-        for source, a, b, to in ((rows, v, u, hout_ref), (cells, vc, uc, cout_ref)):
-            one, two = row_at(source, y, HID)
-            to[y, :, :128] = jnp.where(lane == 0, a, one).astype(BF16)
-            to[y, :, 128:] = jnp.where(lane == 127, b, two).astype(BF16)
-        return tuple(roll(x, 127) for x in state)
-
-    lax.fori_loop(
-        0, ROWS, finish, (roll(edge, 127), roll(edge, 62), roll(edge_cell, 127), roll(edge_cell, 62)), unroll=4
-    )
+                part = there.at[block_at * HID : block_at * HID + HID, where]
+                part[...] = jnp.where(lane == spot, value, part[...])
+
+    for source, columns, to in ((rows, edge, hout_ref), (cells, edge_cell, cout_ref)):
+        for y in range(ROWS):
+            one, two = corners(columns, y, row_at(source, y, HID))
+            to[y, :, :128] = one.astype(BF16)
+            to[y, :, 128:] = two.astype(BF16)
 
     sent = out_buf.at[pl.ds(1, PEERS - 1)]
     pltpu.make_async_remote_copy(
@@ -455,7 +461,7 @@
 ):
     vmem = pl.BlockSpec(memory_space=pltpu.VMEM)
     smem = pl.BlockSpec(memory_space=pltpu.SMEM)
-    hbm = pl.BlockSpec(memory_space=pl.ANY)
+    hbm = pl.BlockSpec(memory_space=pltpu.HBM)
     padded = (ROWS + 2) * COLS
     hidden, memory = pl.pallas_call(
         body,
@@ -478,6 +484,8 @@
             pltpu.VMEM((3 * HID, padded), BF16),
             pltpu.VMEM((3 * CH, padded), BF16),
             pltpu.VMEM((2, ROWS * HID, 128), F32),
+            pltpu.VMEM((128, COLS * BLOCK), F32),
+            pltpu.VMEM((128, COLS * BLOCK), F32),
             pltpu.VMEM((STEPS, 6, HID, 128), BF16),
             pltpu.VMEM((STEPS, 14, HID, 128), BF16),
             pltpu.VMEM((6, CH, 128), BF16),
@@ -489,7 +497,7 @@
             pltpu.SemaphoreType.DMA((STEPS + 1,)),
         ],
         compiler_params=pltpu.CompilerParams(
-            collective_id=0, has_side_effects=True, vmem_limit_bytes=60 * 2**20
+            collective_id=0, has_side_effects=True, vmem_limit_bytes=30 * 2**20
         ),
         name="reproject_and_step",
     )(

time: 69.4 us -> 65.4 us (0.942)
  Pallas kernels: 65.3 us -> 55.4 us
  local copies, waits for them, and re-layouts: 3.27 us -> 8.84 us
    pallas_call x1, Pallas kernels: 65.3 us -> 55.4 us  [on_device(): pl.pallas_call(body, out_shape=[jax.ShapeDtypeStruct((ROWS, HID, COLS), B...]
    unnamed x4 -> x22, local copies, waits for them, and re-layouts: 3.27 us -> 8.84 us
where the time goes in v2:
time: 65.4 us; the launch traced here: 64.9 us
  Pallas kernels  55.4 us (85%)
  local copies, waits for them, and re-layouts  8.84 us (14%)
  between operations  0.68 us (1%)
    pallas_call x1, Pallas kernels, on_device(): pl.pallas_call(body, out_shape=[jax.ShapeDtypeStruct((ROWS, HID, COLS), B...  55.4 us
    unnamed x22, local copies, waits for them, and re-layouts  8.84 us

profile of v2, /device:TPU:1, one launch (start us, length us, event | category | flops | bytes accessed | tf_op | source)
XLA Modules:
  0.0 64.9 jit_solution(9229653626836099347)
XLA Ops:
  0.6 0.0 copy-start.7
  0.6 0.0 copy-start.6
  0.7 0.0 copy-start.8
  0.7 0.0 copy-start.9
  0.7 0.6 copy-done.7
  1.3 0.0 copy-done.6
  1.3 0.0 copy-done.8
  1.3 0.0 copy-done.9
  1.3 0.0 copy-start
  1.3 1.2 %copy-done = bf16[1,128,4,8,128]{4,3,2,1,0:T(8,128)(2,1)S(1)} copy-done((bf16[1,128,4,8,128]{4,3,2,1,0:T(8,128)(2,1)S(1)}, bf16[1,128,4,8,128]{4,3,2,1,0:T(8,128)(2,1)}, u32[]{:S(2)}) %copy-start) | copy-done | bytes 1048600
  2.6 0.0 copy-start.1
  2.6 1.0 %copy-done.1 = bf16[128,16,128]{2,1,0:T(8,128)(2,1)S(1)} copy-done((bf16[128,16,128]{2,1,0:T(8,128)(2,1)S(1)}, bf16[128,16,128]{2,1,0:T(8,128)(2,1)}, u32[]{:S(2)}) %copy-start.1) | copy-done | bytes 524312
  3.6 0.0 copy-start.2
  3.6 1.0 %copy-done.2 = bf16[32,32,256]{2,1,0:T(8,128)(2,1)S(1)} copy-done((bf16[32,32,256]{2,1,0:T(8,128)(2,1)S(1)}, bf16[32,32,256]{2,1,0:T(8,128)(2,1)}, u32[]{:S(2)}) %copy-start.2) | copy-done | bytes 524312
  4.6 0.0 copy-start.3
  4.7 1.0 %copy-done.3 = bf16[32,32,256]{2,1,0:T(8,128)(2,1)S(1)} copy-done((bf16[32,32,256]{2,1,0:T(8,128)(2,1)S(1)}, bf16[32,32,256]{2,1,0:T(8,128)(2,1)}, u32[]{:S(2)}) %copy-start.3) | copy-done | bytes 524312
  5.7 0.0 copy-start.4
  5.7 0.9 %copy-done.4 = bf16[128,288]{0,1:T(8,128)(2,1)S(1)} copy-done((bf16[128,288]{0,1:T(8,128)(2,1)S(1)}, bf16[128,288]{0,1:T(8,128)(2,1)}, u32[]{:S(2)}) %copy-start.4) | copy-done | bytes 73752
  6.6 0.0 copy-start.5
  6.6 0.8 %copy-done.5 = bf16[128,144]{0,1:T(8,128)(2,1)S(1)} copy-done((bf16[128,144]{0,1:T(8,128)(2,1)S(1)}, bf16[128,144]{0,1:T(8,128)(2,1)}, u32[]{:S(2)}) %copy-start.5) | copy-done | bytes 36888
  7.3 55.4 %reproject_and_step.1 = (bf16[32,32,256]{2,1,0:T(8,128)(2,1)S(1)}, bf16[32,32,256]{2,1,0:T(8,128)(2,1)S(1)}) custom-call(s32[1,4,128]{2,1,0:T(4,128)S(1)} %bitcast.13, bf16[128,16,128]{2,1,0:T(8,128)(2,1)S(1)} %copy-done.1, bf16[128,4,8,128]{3,2,1,0:T(8,128)(2,1)S(1)} %bitcast.8, s32[1,4,128]{2,1,0:T(4,128)S(1)} %bitcast.14, s32[1,128]{1,0:T(1,128)S(1)} %copy-done.8, ...), custom_call_target="tpu_custom_call" | custom-call | tf_op jit(solution)/shard_map/reproject_and_step/pallas_call | solution.py:466
  62.8 1.1 %copy.12 = bf16[32,32,256]{2,1,0:T(8,128)(2,1)} copy(bf16[32,32,256]{2,0,1:T(8,128)(2,1)S(1)} %bitcast.10) | data formatting | bytes 1048576
  63.8 1.1 %copy.13 = bf16[32,32,256]{2,1,0:T(8,128)(2,1)} copy(bf16[32,32,256]{2,0,1:T(8,128)(2,1)S(1)} %bitcast.9) | data formatting | bytes 1048576
Async XLA Ops:
  0.6 0.7 %copy-start.7 = (s32[1,128,4]{1,2,0:T(4,128)S(1)}, s32[1,128,4]{1,2,0:T(4,128)}, u32[]{:S(2)}) copy-start(s32[1,128,4]{1,2,0:T(4,128)} %param.13) | copy-start | bytes 6148
  0.6 0.7 %copy-start.6 = (s32[1,128,4]{1,2,0:T(4,128)S(1)}, s32[1,128,4]{1,2,0:T(4,128)}, u32[]{:S(2)}) copy-start(s32[1,128,4]{1,2,0:T(4,128)} %param.11) | copy-start | bytes 6148
  0.7 0.7 %copy-start.8 = (s32[1,128]{1,0:T(1,128)S(1)}, s32[1,128]{1,0:T(1,128)}, u32[]{:S(2)}) copy-start(s32[1,128]{1,0:T(1,128)} %count_ref.1) | copy-start | bytes 1540
  0.7 0.7 %copy-start.9 = (f32[128]{0:T(128)S(1)}, f32[128]{0:T(128)}, u32[]{:S(2)}) copy-start(f32[128]{0:T(128)} %param.17) | copy-start | bytes 1540
  1.3 1.2 %copy-start = (bf16[1,128,4,8,128]{4,3,2,1,0:T(8,128)(2,1)S(1)}, bf16[1,128,4,8,128]{4,3,2,1,0:T(8,128)(2,1)}, u32[]{:S(2)}) copy-start(bf16[1,128,4,8,128]{4,3,2,1,0:T(8,128)(2,1)} %param.12) | copy-start | bytes 3145732
  2.6 1.0 %copy-start.1 = (bf16[128,16,128]{2,1,0:T(8,128)(2,1)S(1)}, bf16[128,16,128]{2,1,0:T(8,128)(2,1)}, u32[]{:S(2)}) copy-start(bf16[128,16,128]{2,1,0:T(8,128)(2,1)} %x_hbm.1) | copy-start | bytes 1572868
  3.6 1.0 %copy-start.2 = (bf16[32,32,256]{2,1,0:T(8,128)(2,1)S(1)}, bf16[32,32,256]{2,1,0:T(8,128)(2,1)}, u32[]{:S(2)}) copy-start(bf16[32,32,256]{2,1,0:T(8,128)(2,1)} %hid_hbm.1) | copy-start | bytes 1572868
  4.6 1.0 %copy-start.3 = (bf16[32,32,256]{2,1,0:T(8,128)(2,1)S(1)}, bf16[32,32,256]{2,1,0:T(8,128)(2,1)}, u32[]{:S(2)}) copy-start(bf16[32,32,256]{2,1,0:T(8,128)(2,1)} %cell_hbm.1) | copy-start | bytes 1572868
  5.7 0.9 %copy-start.4 = (bf16[128,288]{0,1:T(8,128)(2,1)S(1)}, bf16[128,288]{0,1:T(8,128)(2,1)}, u32[]{:S(2)}) copy-start(bf16[128,288]{0,1:T(8,128)(2,1)} %param.16) | copy-start | bytes 221188
  6.6 0.8 %copy-start.5 = (bf16[128,144]{0,1:T(8,128)(2,1)S(1)}, bf16[128,144]{0,1:T(8,128)(2,1)}, u32[]{:S(2)}) copy-start(bf16[128,144]{0,1:T(8,128)(2,1)} %param.15) | copy-start | bytes 110596

commit v3 on v2

--- a/solution.py
+++ b/solution.py
@@ -11,6 +11,7 @@
 
 STEPS = 3
 MESH = pl.DeviceIdType.MESH
+LOGICAL = pl.DeviceIdType.LOGICAL
 F32 = jnp.float32
 BF16 = jnp.bfloat16
 PEERS = 128
@@ -41,27 +42,22 @@
     return (lax.rem(lax.div(j, 2), 4), lax.div(i, 4) * 2 + lax.div(j, 8), lax.rem(i, 4), lax.rem(j, 2))
 
 
-def device_at(x, y, z, c):
-    return lax.div(y, 2) * 4 + z, lax.rem(y, 2) * 8 + x * 2 + c
-
-
 class Places:
     def __init__(self):
         x, y, z, c = coords()
+        ys = [lax.rem(y + d, 4) for d in range(4)]
         self.x = [lax.rem(x + d, 4) * 2 for d in range(4)]
-        ys = [lax.rem(y + d, 4) for d in range(4)]
-        self.y_lat = [lax.div(v, 2) * 4 for v in ys]
-        self.y_lon = [lax.rem(v, 2) * 8 for v in ys]
-        self.z = [lax.rem(z + d, 4) for d in range(4)]
+        self.y = [lax.div(v, 2) * 64 + lax.rem(v, 2) * 8 for v in ys]
+        self.z = [lax.rem(z + d, 4) * 16 for d in range(4)]
         self.c = [lax.rem(c + d, 2) for d in range(2)]
+        self.sums = {}
 
     def __call__(self, offset, sign=1):
         dx, dy, dz, dc = ((sign * d) % m for d, m in zip(offset, (4, 4, 4, 2)))
-        return self.y_lat[dy] + self.z[dz], self.y_lon[dy] + self.x[dx] + self.c[dc]
-
-    def index(self, offset, sign=1):
-        lat, lon = self(offset, sign)
-        return lat * 16 + lon
+        key = (dy, dz, dc)
+        if key not in self.sums:
+            self.sums[key] = self.z[dz] + self.y[dy] + self.c[dc]
+        return self.sums[key] + self.x[dx]
 
 
 def lanes(shape):
@@ -224,26 +220,32 @@
 
 
 def body(
-    stab, x_hbm, w_hbm, target_ref, count_ref, state_ref, input_ref, bias_ref, hid_hbm, cell_hbm,
+    stab_hbm, x_hbm, w_hbm, hid_hbm, cell_hbm, target_hbm, count_hbm, state_hbm, input_hbm, bias_hbm,
     hout_ref, cout_ref,
-    tab, x_ref, w_ref, hid_ref, cell_ref, weight, out_buf, in_buf, wide, sums, rows, s0, s1, fshifted, cells, ga, gb,
+    tab, stab, x_ref, w_ref, hid_ref, cell_ref, target_ref, count_ref, state_ref, input_ref, bias_ref, weight, out_buf, in_buf, wide, sums, rows, s0, s1, fshifted, cells, ga, gb,
     qh, rh, qf, rf, load_sem, far_send, far_recv, near_send, near_recv,
 ):
     loads = [
         pltpu.make_async_copy(a, b, load_sem.at[k])
-        for k, (a, b) in enumerate(((x_hbm, x_ref), (w_hbm, w_ref), (hid_hbm, hid_ref), (cell_hbm, cell_ref)))
+        for k, (a, b) in enumerate(
+            (
+                (stab_hbm, stab), (x_hbm, x_ref), (w_hbm, w_ref), (hid_hbm, hid_ref), (cell_hbm, cell_ref),
+                (target_hbm, target_ref), (count_hbm, count_ref), (state_hbm, state_ref), (input_hbm, input_ref),
+                (bias_hbm, bias_ref),
+            )
+        )
     ]
     for copy in loads:
         copy.start()
     at = Places()
     barrier = pltpu.get_barrier_semaphore()
-    tab[0] = at.index(ORDER[0])
+    tab[0] = at(ORDER[0])
     for offset in sorted(ORDER[1:], key=lambda d: -sum(min(a, 4 - a) for a in d[:3])):
-        pl.semaphore_signal(barrier, inc=1, device_id=at(offset), device_id_type=MESH)
+        pl.semaphore_signal(barrier, inc=1, device_id=at(offset), device_id_type=LOGICAL)
     for n in range(1, PEERS):
-        tab[n] = at.index(ORDER[n])
-    loads[0].wait()
-    loads[1].wait()
+        tab[n] = at(ORDER[n])
+    for copy in loads[:3]:
+        copy.wait()
 
     def one_band(n, carry):
         band(n, out_buf, n, tab, stab, x_ref, w_ref)
@@ -258,7 +260,7 @@
                 send_sem=far_send,
                 recv_sem=far_recv.at[chunk],
                 device_id=at(ORDER[n]),
-                device_id_type=MESH,
+                device_id_type=LOGICAL,
             ).start()
 
     band(0, in_buf, 0, tab, stab, x_ref, w_ref)
@@ -272,7 +274,7 @@
             send(first - GROUP, first)
     send(PEERS - GROUP, PEERS)
 
-    loads[2].wait()
+    loads[3].wait()
     for c in range(HID):
         for half in range(2):
             rows[half, pl.ds(c, ROWS, stride=HID), :] = hid_ref[c, :, half * 128 : half * 128 + 128].astype(F32)
@@ -287,7 +289,8 @@
     state = lax.fori_loop(0, ROWS, prepare, (outer.empty(), inner.empty()), unroll=2)
     edge, near = outer.place(state[0]), inner.place(state[1])
     stage(qh.at[0], row_at(rows, 0, HID), row_at(rows, ROWS - 1, HID), edge, near)
-    loads[3].wait()
+    for copy in loads[4:]:
+        copy.wait()
     for c in range(HID):
         for half in range(2):
             cells[half, pl.ds(c, ROWS, stride=HID), :] = cell_ref[c, :, half * 128 : half * 128 + 128].astype(F32)
@@ -324,7 +327,7 @@
         got = in_buf.at[pl.ds(first, start + size - first)]
         pltpu.make_async_remote_copy(
             src_ref=got, dst_ref=got, send_sem=far_send, recv_sem=far_recv.at[g],
-            device_id=at(ORDER[1]), device_id_type=MESH,
+            device_id=at(ORDER[1]), device_id_type=LOGICAL,
         ).wait_recv()
 
         def unpack(n, carry):
@@ -336,7 +339,7 @@
         which = lax.shift_right_logical(lanes((1, taken)), 2)
         origin = jnp.zeros((1, taken), jnp.int32)
         for n in range(size):
-            origin = jnp.where(which == n, at.index(ORDER[start + n], -1), origin)
+            origin = jnp.where(which == n, at(ORDER[start + n], -1), origin)
         spot = (sublanes((128, taken)) == origin).astype(F32).astype(BF16)
         aims = jnp.dot(aim8, spot, preferred_element_type=F32)
         mine = sublanes((8, taken)) == lanes((8, taken)) % SLOTS
@@ -448,32 +451,45 @@
     sent = out_buf.at[pl.ds(1, PEERS - 1)]
     pltpu.make_async_remote_copy(
         src_ref=sent, dst_ref=sent, send_sem=far_send, recv_sem=far_recv.at[0],
-        device_id=at(ORDER[1]), device_id_type=MESH,
+        device_id=at(ORDER[1]), device_id_type=LOGICAL,
     ).wait_send()
     for t in range(STEPS):
         whole(rh.at[t], near_send.at[t], near_recv.at[t]).wait_send()
     whole(rf, near_send.at[STEPS], near_recv.at[STEPS]).wait_send()
 
 
+def in_hbm(x):
+    return pltpu.with_memory_space_constraint(x, pltpu.HBM)
+
+
 def on_device(
     satellite_blocks, slot_source, slot_weight, slot_target, tile_counts,
     gate_input_weight, gate_state_weight, gate_bias, hidden_init, cell_init,
 ):
+    operands = (
+        slot_source.transpose(0, 2, 1), satellite_blocks, slot_weight[0], hidden_init, cell_init,
+        slot_target.transpose(0, 2, 1), tile_counts, gate_state_weight.T, gate_input_weight.T, gate_bias.reshape(1, -1),
+    )
     vmem = pl.BlockSpec(memory_space=pltpu.VMEM)
-    smem = pl.BlockSpec(memory_space=pltpu.SMEM)
     hbm = pl.BlockSpec(memory_space=pltpu.HBM)
     padded = (ROWS + 2) * COLS
     hidden, memory = pl.pallas_call(
         body,
         out_shape=[jax.ShapeDtypeStruct((ROWS, HID, COLS), BF16)] * 2,
-        in_specs=[smem, hbm, hbm] + [vmem] * 5 + [hbm, hbm],
+        in_specs=[hbm] * 10,
         out_specs=[vmem, vmem],
         scratch_shapes=[
             pltpu.SMEM((PEERS,), jnp.int32),
+            pltpu.SMEM((1, SLOTS, PEERS), jnp.int32),
             pltpu.VMEM((PEERS, CH, 128), BF16),
             pltpu.VMEM((PEERS, SLOTS, 8, 128), BF16),
             pltpu.VMEM((HID, ROWS, COLS), BF16),
             pltpu.VMEM((HID, ROWS, COLS), BF16),
+            pltpu.VMEM((1, SLOTS, PEERS), jnp.int32),
+            pltpu.VMEM((1, PEERS), jnp.int32),
+            pltpu.VMEM((9 * HID, 128), BF16),
+            pltpu.VMEM((9 * CH, 128), BF16),
+            pltpu.VMEM((1, 128), F32),
             pltpu.VMEM((128, 512), BF16),
             pltpu.VMEM((PEERS, SLOTS, CH, 128), BF16),
             pltpu.VMEM((PEERS, SLOTS, CH, 128), BF16),
@@ -490,7 +506,7 @@
             pltpu.VMEM((STEPS, 14, HID, 128), BF16),
             pltpu.VMEM((6, CH, 128), BF16),
             pltpu.VMEM((14, CH, 128), BF16),
-            pltpu.SemaphoreType.DMA((4,)),
+            pltpu.SemaphoreType.DMA((10,)),
             pltpu.SemaphoreType.DMA,
             pltpu.SemaphoreType.DMA((len(SIZES),)),
             pltpu.SemaphoreType.DMA((STEPS + 1,)),
@@ -500,10 +516,7 @@
             collective_id=0, has_side_effects=True, vmem_limit_bytes=30 * 2**20
         ),
         name="reproject_and_step",
-    )(
-        slot_source.transpose(0, 2, 1), satellite_blocks, slot_weight[0], slot_target.transpose(0, 2, 1), tile_counts,
-        gate_state_weight.T, gate_input_weight.T, gate_bias.reshape(1, -1), hidden_init, cell_init,
-    )
+    )(*[in_hbm(v) for v in operands])
     return hidden.transpose(1, 0, 2), memory.transpose(1, 0, 2)
 
 

time: 65.4 us -> 57.7 us (0.88)
  local copies, waits for them, and re-layouts: 8.84 us -> 2.17 us
  Pallas kernels: 55.4 us -> 54.7 us
    unnamed x22 -> x2, local copies, waits for them, and re-layouts: 8.84 us -> 2.17 us
    pallas_call x1, Pallas kernels: 55.4 us -> 54.7 us  [on_device(): pl.pallas_call(body, out_shape=[jax.ShapeDtypeStruct((ROWS, HID, COLS), B...]
where the time goes in v3:
time: 57.7 us; the launch traced here: 57.5 us
  Pallas kernels  54.7 us (95%)
  local copies, waits for them, and re-layouts  2.17 us (4%)
  between operations  0.64 us (1%)
    pallas_call x1, Pallas kernels, on_device(): pl.pallas_call(body, out_shape=[jax.ShapeDtypeStruct((ROWS, HID, COLS), B...  54.7 us
    unnamed x2, local copies, waits for them, and re-layouts  2.17 us

profile of v3, /device:TPU:1, one launch (start us, length us, event | category | flops | bytes accessed | tf_op | source)
XLA Modules:
  0.0 57.5 jit_solution(14056461115813944021)
XLA Ops:
  0.6 54.7 %reproject_and_step.1 = (bf16[32,32,256]{2,1,0:T(8,128)(2,1)S(1)}, bf16[32,32,256]{2,1,0:T(8,128)(2,1)S(1)}) custom-call(s32[1,4,128]{2,1,0:T(4,128)} %bitcast.13, bf16[128,16,128]{2,1,0:T(8,128)(2,1)} %x_hbm.1, bf16[128,4,8,128]{3,2,1,0:T(8,128)(2,1)} %bitcast.10, bf16[32,32,256]{2,1,0:T(8,128)(2,1)} %hid_hbm.1, bf16[32,32,256]{2,1,0:T(8,128)(2,1)} %cell_hbm.1, ...), custom_call_target="tpu_custom_call" | custom-call | tf_op jit(solution)/shard_map/reproject_and_step/pallas_call | solution.py:476
  55.4 1.1 %copy.12 = bf16[32,32,256]{2,1,0:T(8,128)(2,1)} copy(bf16[32,32,256]{2,0,1:T(8,128)(2,1)S(1)} %bitcast.9) | data formatting | bytes 1048576
  56.5 1.1 %copy.13 = bf16[32,32,256]{2,1,0:T(8,128)(2,1)} copy(bf16[32,32,256]{2,0,1:T(8,128)(2,1)S(1)} %bitcast.8) | data formatting | bytes 1048576

commit v4 on v3

--- a/solution.py
+++ b/solution.py
@@ -21,6 +21,7 @@
 GROUP = 8
 BARRIER_AT = 16
 BLOCK = 5
+HALO = 3
 ROWS = 32
 COLS = 256
 CH = 16
@@ -99,7 +100,7 @@
 
 
 def padded_at(y):
-    return (y + 1) * COLS if isinstance(y, int) else pl.multiple_of((y + 1) * COLS, COLS)
+    return (y + HALO) * COLS if isinstance(y, int) else pl.multiple_of((y + HALO) * COLS, COLS)
 
 
 class Picker:
@@ -117,49 +118,60 @@
             jnp.where(lane == self.right, halves[1], roll(state[1], 1)),
         )
 
-    def place(self, state):
+    def place(self, state, lowest=0):
         lane = lanes(self.shape)
-        left = roll(state[0], (1 - self.left) % 128)
-        right = roll(state[1], (65 - self.right) % 128)
-        return jnp.where((lane >= 1) & (lane <= 32), left, jnp.where((lane >= 65) & (lane <= 96), right, 0.0))
+        left = roll(state[0], (lowest + HALO - self.left) % 128)
+        right = roll(state[1], (lowest + HALO + 64 - self.right) % 128)
+        first, last = lowest + HALO, HALO + ROWS - 1
+        return jnp.where(
+            (lane >= first) & (lane <= last),
+            left,
+            jnp.where((lane >= first + 64) & (lane <= last + 64), right, 0.0),
+        )
+
+    def insert(self, value, y, halves):
+        lane = lanes(self.shape)
+        at = y + HALO
+        value = jnp.where(lane == at, roll(halves[0], (at - self.left) % 128), value)
+        return jnp.where(lane == at + 64, roll(halves[1], (at + 64 - self.right) % 128), value)
 
 
 def corners(edge, y, halves):
     lane = lanes(edge.shape)
-    left = roll(edge, (-(y + 1)) % 128)
-    right = roll(edge, (62 - y) % 128)
+    left = roll(edge, (-(y + HALO)) % 128)
+    right = roll(edge, (63 - HALO - y) % 128)
     return jnp.where(lane == 0, left, halves[0]), jnp.where(lane == 127, right, halves[1])
 
 
-def stage(q_ref, top, bottom, edge, near):
-    for k, v in enumerate((top[0], top[1], edge, near, bottom[0], bottom[1])):
+def stage(q_ref, row_of, depth, columns):
+    top = [h for y in range(depth) for h in row_of(y)]
+    bottom = [h for y in range(ROWS - depth, ROWS) for h in row_of(y)]
+    for k, v in enumerate((*top, *columns, *bottom)):
         q_ref[k] = v.astype(BF16)
 
 
-def swap(q_ref, r_ref, send_sem, recv_sem):
+def swap(plan, q_ref, r_ref, send_sem, recv_sem):
     i = lax.axis_index("lat")
     j = lax.axis_index("lon")
-    up, down = lax.rem(i + 7, 8), lax.rem(i + 1, 8)
-    left, right = lax.rem(j + 15, 16), lax.rem(j + 1, 16)
-    plan = (
-        ((up, j), 0, 4, 4),
-        ((down, j), 2, 4, 0),
-        ((i, left), 2, 1, 9),
-        ((i, right), 2, 1, 8),
-        ((up, left), 2, 1, 13),
-        ((up, right), 2, 1, 12),
-        ((down, left), 2, 1, 11),
-        ((down, right), 2, 1, 10),
-    )
-    for target, source, size, slot in plan:
+    lat = {0: i, -1: lax.rem(i + 7, 8), 1: lax.rem(i + 1, 8)}
+    lon = {0: j, -1: lax.rem(j + 15, 16), 1: lax.rem(j + 1, 16)}
+    for di, dj, source, size, slot in plan:
         pltpu.make_async_remote_copy(
             src_ref=q_ref.at[pl.ds(source, size)],
             dst_ref=r_ref.at[pl.ds(slot, size)],
             send_sem=send_sem,
             recv_sem=recv_sem,
-            device_id=target,
+            device_id=(lat[di], lon[dj]),
             device_id_type=MESH,
         ).start()
+
+
+DEEP = (
+    (-1, 0, 0, 8, 8), (1, 0, 6, 8, 0), (0, -1, 6, 1, 17), (0, 1, 6, 1, 16),
+    (-1, -1, 6, 1, 21), (-1, 1, 6, 1, 20), (1, -1, 6, 1, 19), (1, 1, 6, 1, 18),
+)
+CELLS = ((-1, 0, 0, 5, 5), (1, 0, 4, 5, 0))
+SIDES = ((0, -1, 0, 1, 1), (0, 1, 0, 1, 0))
 
 
 def whole(r_ref, send_sem, recv_sem):
@@ -174,37 +186,40 @@
     )
 
 
-def edge_inputs(edge, near, r_ref, count):
+def in_globe(y):
     i = lax.axis_index("lat")
+    return ((y >= 0) | (i > 0)) & ((y < ROWS) | (i < 7))
+
+
+def frame(count, middle, above, below):
     lane = lanes((count, 128))
-    half = lane < 64
-    place = jnp.where(half, lane, lane - 64)
-    top = (place == 0) & (i > 0)
-    bottom = (place == 33) & (i < 7)
-    middle = (place >= 1) & (place <= 32)
-    got = lambda k: r_ref[k].astype(F32)
-
-    def frame(mid, above, below):
-        return jnp.where(middle, mid, jnp.where(top, above, jnp.where(bottom, below, 0.0)))
-
-    edges = frame(edge, roll(got(0), 96), roll(got(6), 32))
-    nears = frame(near, roll(got(1), 96), roll(got(7), 32))
-    sides = frame(
-        jnp.where(half, roll(got(8), 64), roll(got(9), 64)),
-        jnp.where(half, roll(got(10), 32), roll(got(11), 32)),
-        jnp.where(half, roll(got(12), 96), roll(got(13), 96)),
-    )
+    y = jnp.where(lane < 64, lane, lane - 64) - HALO
+    live = in_globe(y) & (y < ROWS + HALO)
+    picked = jnp.where(y < 0, roll(above, 96), jnp.where(y < ROWS, middle, roll(below, 32)))
+    return jnp.where(live, picked, 0.0)
+
+
+def taps_of(edges, nears, sides):
+    half = lanes(edges.shape) < 64
     three = (jnp.where(half, sides, nears), edges, jnp.where(half, nears, sides))
     above = [roll(v, 1) for v in three]
     below = [roll(v, 127) for v in three]
     return jnp.concatenate([v.astype(BF16) for v in (*above, *three, *below)], axis=0)
 
 
+def deep_taps(edge, near, r_ref, count):
+    got = lambda k: r_ref[k].astype(F32)
+    half = lanes((count, 128)) < 64
+    swapped = [roll(jnp.where(half, got(k + 1), got(k)), 64) for k in (16, 18, 20)]
+    return taps_of(
+        frame(count, edge, got(0), got(14)), frame(count, near, got(1), got(15)), frame(count, *swapped)
+    )
+
+
 def halo_rows(r_ref, into, count):
-    i = lax.axis_index("lat")
-    for slot, live, at in ((2, i > 0, 0), (4, i < 7, (ROWS + 1) * COLS)):
-        halves = [jnp.where(live, r_ref[slot + k].astype(F32), 0.0) for k in range(2)]
-        spread(halves, into, count, at)
+    for slot, y in ((2, -3), (4, -2), (6, -1), (8, 32), (10, 33), (12, 34)):
+        halves = [jnp.where(in_globe(y), r_ref[slot + k].astype(F32), 0.0) for k in range(2)]
+        spread(halves, into, count, padded_at(y))
 
 
 def update(gates, memory):
@@ -223,7 +238,7 @@
     stab_hbm, x_hbm, w_hbm, hid_hbm, cell_hbm, target_hbm, count_hbm, state_hbm, input_hbm, bias_hbm,
     hout_ref, cout_ref,
     tab, stab, x_ref, w_ref, hid_ref, cell_ref, target_ref, count_ref, state_ref, input_ref, bias_ref, weight, out_buf, in_buf, wide, sums, rows, s0, s1, fshifted, cells, ga, gb,
-    qh, rh, qf, rf, load_sem, far_send, far_recv, near_send, near_recv,
+    qh, rh, qe, re, qf, rf, qc, rc, load_sem, far_send, far_recv, near_send, near_recv,
 ):
     loads = [
         pltpu.make_async_copy(a, b, load_sem.at[k])
@@ -288,18 +303,21 @@
 
     state = lax.fori_loop(0, ROWS, prepare, (outer.empty(), inner.empty()), unroll=2)
     edge, near = outer.place(state[0]), inner.place(state[1])
-    stage(qh.at[0], row_at(rows, 0, HID), row_at(rows, ROWS - 1, HID), edge, near)
+    stage(qh, lambda y: row_at(rows, y, HID), HALO, (edge, near))
+    swap(DEEP, qh, rh, near_send.at[0], near_recv.at[0])
     for copy in loads[4:]:
         copy.wait()
     for c in range(HID):
         for half in range(2):
-            cells[half, pl.ds(c, ROWS, stride=HID), :] = cell_ref[c, :, half * 128 : half * 128 + 128].astype(F32)
-    swap(qh.at[0], rh.at[0], near_send.at[0], near_recv.at[0])
+            cells[half, pl.ds(c + 2 * HID, ROWS, stride=HID), :] = cell_ref[c, :, half * 128 : half * 128 + 128].astype(F32)
 
     def prepare_cell(k, state):
-        return outer.take(state, row_at(cells, ROWS - 1 - k, HID))
+        return outer.take(state, row_at(cells, ROWS + 1 - k, HID))
 
     edge_cell = outer.place(lax.fori_loop(0, ROWS, prepare_cell, outer.empty(), unroll=2))
+
+    stage(qc, lambda y: row_at(cells, y + 2, HID), 2, (edge_cell,))
+    swap(CELLS, qc, rc, near_send.at[STEPS + 1], near_recv.at[STEPS + 1])
 
     scale = jnp.where(sublanes((128, 1)) < 3 * HID, 0.5, 1.0)
     bias = jnp.sum(jnp.where(sublanes((128, 128)) == lanes((128, 128)), bias_ref[...], 0.0), axis=1, keepdims=True)
@@ -354,17 +372,15 @@
     def cell_row(y):
         return sums[pl.ds(2 * y, CH, stride=64), :], sums[pl.ds(2 * y + 1, CH, stride=64), :]
 
-    spot = lanes((CH, 128))
+    fouter, finner = Picker(0, 127, CH), Picker(1, 126, CH)
     fedge = fnear = jnp.zeros((CH, 128), F32)
     for y in range(ROWS):
         halves = cell_row(y)
         spread(halves, fshifted, CH, padded_at(y))
-        fedge = jnp.where(spot == y + 1, roll(halves[0], y + 1), fedge)
-        fedge = jnp.where(spot == y + 65, roll(halves[1], (y + 66) % 128), fedge)
-        fnear = jnp.where(spot == y + 1, roll(halves[0], y), fnear)
-        fnear = jnp.where(spot == y + 65, roll(halves[1], (y + 67) % 128), fnear)
-    stage(qf, cell_row(0), cell_row(ROWS - 1), fedge, fnear)
-    swap(qf, rf, near_send.at[STEPS], near_recv.at[STEPS])
+        fedge = fouter.insert(fedge, y, halves)
+        fnear = finner.insert(fnear, y, halves)
+    stage(qf, cell_row, HALO, (fedge, fnear))
+    swap(DEEP, qf, rf, near_send.at[STEPS], near_recv.at[STEPS])
 
     fmini = None
     for t in range(STEPS):
@@ -378,14 +394,15 @@
             return jnp.dot(weight[:, :448], rhs, preferred_element_type=F32)
 
         def finish_row(y, gates):
-            hidden, memory = update(gates, jnp.concatenate(row_at(cells, y, HID), axis=1))
+            hidden, memory = update(gates, jnp.concatenate(row_at(cells, y + 2, HID), axis=1))
+            if not (isinstance(y, int) and 0 <= y < ROWS):
+                hidden = jnp.where(in_globe(y), hidden, 0.0) if isinstance(y, int) else hidden
             halves = halves_of(hidden)
-            where = pl.ds(pl.multiple_of(y * HID, HID), HID)
             for half, v in enumerate(halves_of(memory)):
-                cells[half, where] = v
+                cells[half, pl.ds(pl.multiple_of((y + 2) * HID, HID), HID)] = v
             if last:
                 for half, v in enumerate(halves):
-                    rows[half, where] = v
+                    rows[half, pl.ds(pl.multiple_of(y * HID, HID), HID)] = v
             else:
                 spread(halves, there, HID, padded_at(y))
             return halves
@@ -407,34 +424,47 @@
         state = 0 if last else inner.empty()
         state = lax.fori_loop(0, (ROWS - 2) // (2 * BLOCK), inside, state)
 
-        whole(rh.at[t], near_send.at[t], near_recv.at[t]).wait_recv()
         if t == 0:
-            whole(rf, near_send.at[STEPS], near_recv.at[STEPS]).wait_recv()
-            fmini = edge_inputs(fedge, fnear, rf, CH)
+            for k, got in ((0, rh), (STEPS + 1, rc), (STEPS, rf)):
+                whole(got, near_send.at[k], near_recv.at[k]).wait_recv()
+            halo_rows(rh, here, HID)
             halo_rows(rf, fshifted, CH)
-        mini = jnp.concatenate([edge_inputs(edge, near, rh.at[t], HID), fmini, ones[:, :128]], axis=0)
-        halo_rows(rh.at[t], here, HID)
+            for slot, y in ((1, -2), (3, -1), (5, 32), (7, 33)):
+                for half in range(2):
+                    cells[half, (y + 2) * HID : (y + 3) * HID] = rc[slot + half].astype(F32)
+            edge_cell = frame(HID, edge_cell, rc[0].astype(F32), rc[9].astype(F32))
+            fmini = deep_taps(fedge, fnear, rf, CH)
+        depth = STEPS - t
+        low, high = gates_of(1 - depth, depth), gates_of(ROWS - 1, depth)
+        above = [finish_row(-r, low[:, (depth - 1 - r) * COLS : (depth - r) * COLS]) for r in range(depth)]
+        below = [finish_row(ROWS - 1 + r, high[:, r * COLS : (r + 1) * COLS]) for r in range(depth)]
+        if t == 0:
+            mini = deep_taps(edge, near, rh, HID)
+        else:
+            whole(re.at[t - 1], near_send.at[t], near_recv.at[t]).wait_recv()
+            half = lanes((HID, 128)) < 64
+            sides = roll(jnp.where(half, re[t - 1, 1].astype(F32), re[t - 1, 0].astype(F32)), 64)
+            mini = taps_of(edge, near, sides)
+        mini = jnp.concatenate([mini, fmini, ones[:, :128]], axis=0)
         gates = jnp.dot(weight[:, :448], mini, preferred_element_type=F32)
         edge, edge_cell = update(gates, edge_cell)
-        tops, bottoms = gates_of(0), gates_of(ROWS - 1)
-        top = finish_row(0, tops)
-        bottom = finish_row(ROWS - 1, bottoms)
         if last:
             break
-        state = inner.take(state, top)
-        far_left = roll(bottom[0], 31)
-        far_right = roll(bottom[1], (96 - 126) % 128)
-        spot = lanes((HID, 128))
-        near = jnp.where(spot == 32, far_left, jnp.where(spot == 96, far_right, inner.place(state)))
-        stage(qh.at[t + 1], corners(edge, 0, top), corners(edge, ROWS - 1, bottom), edge, near)
-        swap(qh.at[t + 1], rh.at[t + 1], near_send.at[t + 1], near_recv.at[t + 1])
-
         lane = lanes((HID, 128))
-        left = [roll(edge, -y % 128).astype(BF16) for y in range(ROWS + 1)]
-        right = [roll(edge, (62 - y) % 128).astype(BF16) for y in range(ROWS + 1)]
-        for y in range(ROWS):
-            first = pl.ds((y + 1) * COLS, 128)
-            second = pl.ds((y + 1) * COLS + 128, 128)
+        edge = jnp.where(in_globe(jnp.where(lane < 64, lane, lane - 64) - HALO), edge, 0.0)
+        qe[t, 0] = edge.astype(BF16)
+        for halves in above:
+            state = inner.take(state, halves)
+        near = inner.place(state, 1 - depth)
+        near = jnp.where((lane == 34) | (lane == 98), 0.0, near)
+        for r, halves in enumerate(below):
+            near = inner.insert(near, ROWS - 1 + r, halves)
+        left = {y: roll(edge, (1 - HALO - y) % 128).astype(BF16) for y in range(1 - depth, ROWS + depth)}
+        right = {y: roll(edge, (63 - HALO - y) % 128).astype(BF16) for y in range(1 - depth, ROWS + depth)}
+        swap(SIDES, qe.at[t], re.at[t], near_send.at[t + 1], near_recv.at[t + 1])
+        for y in range(1 - depth, ROWS + depth - 1):
+            first = pl.ds(padded_at(y), 128)
+            second = pl.ds(padded_at(y) + 128, 128)
             for block_at, where, spot, value in (
                 (0, first, 1, left[y]), (1, first, 0, left[y + 1]),
                 (1, second, 127, right[y]), (2, second, 126, right[y + 1]),
@@ -442,9 +472,9 @@
                 part = there.at[block_at * HID : block_at * HID + HID, where]
                 part[...] = jnp.where(lane == spot, value, part[...])
 
-    for source, columns, to in ((rows, edge, hout_ref), (cells, edge_cell, cout_ref)):
+    for source, skip, columns, to in ((rows, 0, edge, hout_ref), (cells, 2, edge_cell, cout_ref)):
         for y in range(ROWS):
-            one, two = corners(columns, y, row_at(source, y, HID))
+            one, two = corners(columns, y, row_at(source, y + skip, HID))
             to[y, :, :128] = one.astype(BF16)
             to[y, :, 128:] = two.astype(BF16)
 
@@ -453,9 +483,8 @@
         src_ref=sent, dst_ref=sent, send_sem=far_send, recv_sem=far_recv.at[0],
         device_id=at(ORDER[1]), device_id_type=LOGICAL,
     ).wait_send()
-    for t in range(STEPS):
-        whole(rh.at[t], near_send.at[t], near_recv.at[t]).wait_send()
-    whole(rf, near_send.at[STEPS], near_recv.at[STEPS]).wait_send()
+    for k, got in ((0, rh), (1, re.at[0]), (2, re.at[1]), (STEPS, rf), (STEPS + 1, rc)):
+        whole(got, near_send.at[k], near_recv.at[k]).wait_send()
 
 
 def in_hbm(x):
@@ -472,7 +501,7 @@
     )
     vmem = pl.BlockSpec(memory_space=pltpu.VMEM)
     hbm = pl.BlockSpec(memory_space=pltpu.HBM)
-    padded = (ROWS + 2) * COLS
+    padded = (ROWS + 2 * HALO) * COLS
     hidden, memory = pl.pallas_call(
         body,
         out_shape=[jax.ShapeDtypeStruct((ROWS, HID, COLS), BF16)] * 2,
@@ -499,18 +528,22 @@
             pltpu.VMEM((3 * HID, padded), BF16),
             pltpu.VMEM((3 * HID, padded), BF16),
             pltpu.VMEM((3 * CH, padded), BF16),
-            pltpu.VMEM((2, ROWS * HID, 128), F32),
+            pltpu.VMEM((2, (ROWS + 4) * HID, 128), F32),
             pltpu.VMEM((128, COLS * BLOCK), F32),
             pltpu.VMEM((128, COLS * BLOCK), F32),
-            pltpu.VMEM((STEPS, 6, HID, 128), BF16),
-            pltpu.VMEM((STEPS, 14, HID, 128), BF16),
-            pltpu.VMEM((6, CH, 128), BF16),
+            pltpu.VMEM((14, HID, 128), BF16),
+            pltpu.VMEM((22, HID, 128), BF16),
+            pltpu.VMEM((2, 1, HID, 128), BF16),
+            pltpu.VMEM((2, 2, HID, 128), BF16),
             pltpu.VMEM((14, CH, 128), BF16),
+            pltpu.VMEM((22, CH, 128), BF16),
+            pltpu.VMEM((9, HID, 128), BF16),
+            pltpu.VMEM((10, HID, 128), BF16),
             pltpu.SemaphoreType.DMA((10,)),
             pltpu.SemaphoreType.DMA,
             pltpu.SemaphoreType.DMA((len(SIZES),)),
-            pltpu.SemaphoreType.DMA((STEPS + 1,)),
-            pltpu.SemaphoreType.DMA((STEPS + 1,)),
+            pltpu.SemaphoreType.DMA((STEPS + 2,)),
+            pltpu.SemaphoreType.DMA((STEPS + 2,)),
         ],
         compiler_params=pltpu.CompilerParams(
             collective_id=0, has_side_effects=True, vmem_limit_bytes=30 * 2**20

time: 57.7 us -> 53.7 us (0.931)
  Pallas kernels: 54.7 us -> 50.8 us
    pallas_call x1, Pallas kernels: 54.7 us -> 50.8 us  [on_device(): pl.pallas_call(body, out_shape=[jax.ShapeDtypeStruct((ROWS, HID, COLS), B...]
where the time goes in v4:
time: 53.7 us; the launch traced here: 53.6 us
  Pallas kernels  50.8 us (95%)
  local copies, waits for them, and re-layouts  2.17 us (4%)
  between operations  0.64 us (1%)
    pallas_call x1, Pallas kernels, on_device(): pl.pallas_call(body, out_shape=[jax.ShapeDtypeStruct((ROWS, HID, COLS), B...  50.8 us
    unnamed x2, local copies, waits for them, and re-layouts  2.17 us

profile of v4, /device:TPU:1, one launch (start us, length us, event | category | flops | bytes accessed | tf_op | source)
XLA Modules:
  0.0 53.6 jit_solution(5711672118168648864)
XLA Ops:
  0.6 50.8 %reproject_and_step.1 = (bf16[32,32,256]{2,1,0:T(8,128)(2,1)S(1)}, bf16[32,32,256]{2,1,0:T(8,128)(2,1)S(1)}) custom-call(s32[1,4,128]{2,1,0:T(4,128)} %bitcast.13, bf16[128,16,128]{2,1,0:T(8,128)(2,1)} %x_hbm.1, bf16[128,4,8,128]{3,2,1,0:T(8,128)(2,1)} %bitcast.10, bf16[32,32,256]{2,1,0:T(8,128)(2,1)} %hid_hbm.1, bf16[32,32,256]{2,1,0:T(8,128)(2,1)} %cell_hbm.1, ...), custom_call_target="tpu_custom_call" | custom-call | tf_op jit(solution)/shard_map/reproject_and_step/pallas_call | solution.py:505
  51.4 1.1 %copy.12 = bf16[32,32,256]{2,1,0:T(8,128)(2,1)} copy(bf16[32,32,256]{2,0,1:T(8,128)(2,1)S(1)} %bitcast.9) | data formatting | bytes 1048576
  52.5 1.1 %copy.13 = bf16[32,32,256]{2,1,0:T(8,128)(2,1)} copy(bf16[32,32,256]{2,0,1:T(8,128)(2,1)S(1)} %bitcast.8) | data formatting | bytes 1048576

commit v5 on v4

--- a/solution.py
+++ b/solution.py
@@ -20,7 +20,6 @@
 STARTS = (0, 64, 96, 112)
 GROUP = 8
 BARRIER_AT = 16
-BLOCK = 5
 HALO = 3
 ROWS = 32
 COLS = 256
@@ -118,11 +117,11 @@
             jnp.where(lane == self.right, halves[1], roll(state[1], 1)),
         )
 
-    def place(self, state, lowest=0):
+    def place(self, state, lowest=0, highest=ROWS - 1):
         lane = lanes(self.shape)
         left = roll(state[0], (lowest + HALO - self.left) % 128)
         right = roll(state[1], (lowest + HALO + 64 - self.right) % 128)
-        first, last = lowest + HALO, HALO + ROWS - 1
+        first, last = lowest + HALO, highest + HALO
         return jnp.where(
             (lane >= first) & (lane <= last),
             left,
@@ -134,13 +133,6 @@
         at = y + HALO
         value = jnp.where(lane == at, roll(halves[0], (at - self.left) % 128), value)
         return jnp.where(lane == at + 64, roll(halves[1], (at + 64 - self.right) % 128), value)
-
-
-def corners(edge, y, halves):
-    lane = lanes(edge.shape)
-    left = roll(edge, (-(y + HALO)) % 128)
-    right = roll(edge, (63 - HALO - y) % 128)
-    return jnp.where(lane == 0, left, halves[0]), jnp.where(lane == 127, right, halves[1])
 
 
 def stage(q_ref, row_of, depth, columns):
@@ -376,11 +368,12 @@
     fedge = fnear = jnp.zeros((CH, 128), F32)
     for y in range(ROWS):
         halves = cell_row(y)
-        spread(halves, fshifted, CH, padded_at(y))
         fedge = fouter.insert(fedge, y, halves)
         fnear = finner.insert(fnear, y, halves)
     stage(qf, cell_row, HALO, (fedge, fnear))
     swap(DEEP, qf, rf, near_send.at[STEPS], near_recv.at[STEPS])
+    for y in range(ROWS):
+        spread(cell_row(y), fshifted, CH, padded_at(y))
 
     fmini = None
     for t in range(STEPS):
@@ -399,30 +392,27 @@
                 hidden = jnp.where(in_globe(y), hidden, 0.0) if isinstance(y, int) else hidden
             halves = halves_of(hidden)
             for half, v in enumerate(halves_of(memory)):
-                cells[half, pl.ds(pl.multiple_of((y + 2) * HID, HID), HID)] = v
-            if last:
-                for half, v in enumerate(halves):
-                    rows[half, pl.ds(pl.multiple_of(y * HID, HID), HID)] = v
-            else:
+                if last:
+                    part = slice(half * 128, half * 128 + 128)
+                    hout_ref[y, :, part] = halves[half].astype(BF16)
+                    cout_ref[y, :, part] = v.astype(BF16)
+                else:
+                    cells[half, (y + 2) * HID : (y + 3) * HID] = v
+            if not last:
                 spread(halves, there, HID, padded_at(y))
             return halves
 
-        def block(low, buffer, state):
-            for r in range(BLOCK - 1, -1, -1):
-                halves = finish_row(low + r, buffer[:, r * COLS : r * COLS + COLS])
+        depth = STEPS - t
+        lowest, highest = (1, ROWS - 2) if t == 0 else (1 - depth, ROWS - 2 + depth)
+        count = (highest - lowest + 1) // 2
+        wide_gates = count * COLS
+        state = inner.empty()
+        ga[:, :wide_gates] = gates_of(lowest + count, count)
+        gb[:, :wide_gates] = gates_of(lowest, count)
+        for buffer, start in ((ga, lowest + count), (gb, lowest)):
+            for r in range(count - 1, -1, -1):
+                halves = finish_row(start + r, buffer[:, r * COLS : r * COLS + COLS])
                 state = state if last else inner.take(state, halves)
-            return state
-
-        def inside(k, state):
-            low = ROWS - 1 - BLOCK - 2 * BLOCK * k
-            gb[...] = gates_of(low - BLOCK, BLOCK)
-            state = block(low, ga, state)
-            ga[...] = gates_of(lax.max(low - 2 * BLOCK, 1), BLOCK)
-            return block(low - BLOCK, gb, state)
-
-        ga[...] = gates_of(ROWS - 1 - BLOCK, BLOCK)
-        state = 0 if last else inner.empty()
-        state = lax.fori_loop(0, (ROWS - 2) // (2 * BLOCK), inside, state)
 
         if t == 0:
             for k, got in ((0, rh), (STEPS + 1, rc), (STEPS, rf)):
@@ -434,11 +424,9 @@
                     cells[half, (y + 2) * HID : (y + 3) * HID] = rc[slot + half].astype(F32)
             edge_cell = frame(HID, edge_cell, rc[0].astype(F32), rc[9].astype(F32))
             fmini = deep_taps(fedge, fnear, rf, CH)
-        depth = STEPS - t
-        low, high = gates_of(1 - depth, depth), gates_of(ROWS - 1, depth)
-        above = [finish_row(-r, low[:, (depth - 1 - r) * COLS : (depth - r) * COLS]) for r in range(depth)]
-        below = [finish_row(ROWS - 1 + r, high[:, r * COLS : (r + 1) * COLS]) for r in range(depth)]
-        if t == 0:
+            low, high = gates_of(1 - depth, depth), gates_of(ROWS - 1, depth)
+            above = [finish_row(-r, low[:, (depth - 1 - r) * COLS : (depth - r) * COLS]) for r in range(depth)]
+            below = [finish_row(ROWS - 1 + r, high[:, r * COLS : (r + 1) * COLS]) for r in range(depth)]
             mini = deep_taps(edge, near, rh, HID)
         else:
             whole(re.at[t - 1], near_send.at[t], near_recv.at[t]).wait_recv()
@@ -453,12 +441,13 @@
         lane = lanes((HID, 128))
         edge = jnp.where(in_globe(jnp.where(lane < 64, lane, lane - 64) - HALO), edge, 0.0)
         qe[t, 0] = edge.astype(BF16)
-        for halves in above:
-            state = inner.take(state, halves)
-        near = inner.place(state, 1 - depth)
-        near = jnp.where((lane == 34) | (lane == 98), 0.0, near)
-        for r, halves in enumerate(below):
-            near = inner.insert(near, ROWS - 1 + r, halves)
+        if t == 0:
+            for halves in above:
+                state = inner.take(state, halves)
+        near = inner.place(state, 1 - depth, highest)
+        if t == 0:
+            for r, halves in enumerate(below):
+                near = inner.insert(near, ROWS - 1 + r, halves)
         left = {y: roll(edge, (1 - HALO - y) % 128).astype(BF16) for y in range(1 - depth, ROWS + depth)}
         right = {y: roll(edge, (63 - HALO - y) % 128).astype(BF16) for y in range(1 - depth, ROWS + depth)}
         swap(SIDES, qe.at[t], re.at[t], near_send.at[t + 1], near_recv.at[t + 1])
@@ -472,11 +461,13 @@
                 part = there.at[block_at * HID : block_at * HID + HID, where]
                 part[...] = jnp.where(lane == spot, value, part[...])
 
-    for source, skip, columns, to in ((rows, 0, edge, hout_ref), (cells, 2, edge_cell, cout_ref)):
+    lane = lanes((HID, 128))
+    for columns, to in ((edge, hout_ref), (edge_cell, cout_ref)):
         for y in range(ROWS):
-            one, two = corners(columns, y, row_at(source, y + skip, HID))
-            to[y, :, :128] = one.astype(BF16)
-            to[y, :, 128:] = two.astype(BF16)
+            left = roll(columns, (-(y + HALO)) % 128).astype(BF16)
+            right = roll(columns, (63 - HALO - y) % 128).astype(BF16)
+            to[y, :, :128] = jnp.where(lane == 0, left, to[y, :, :128])
+            to[y, :, 128:] = jnp.where(lane == 127, right, to[y, :, 128:])
 
     sent = out_buf.at[pl.ds(1, PEERS - 1)]
     pltpu.make_async_remote_copy(
@@ -529,8 +520,8 @@
             pltpu.VMEM((3 * HID, padded), BF16),
             pltpu.VMEM((3 * CH, padded), BF16),
             pltpu.VMEM((2, (ROWS + 4) * HID, 128), F32),
-            pltpu.VMEM((128, COLS * BLOCK), F32),
-            pltpu.VMEM((128, COLS * BLOCK), F32),
+            pltpu.VMEM((128, COLS * (ROWS // 2 + 1)), F32),
+            pltpu.VMEM((128, COLS * (ROWS // 2 + 1)), F32),
             pltpu.VMEM((14, HID, 128), BF16),
             pltpu.VMEM((22, HID, 128), BF16),
             pltpu.VMEM((2, 1, HID, 128), BF16),

time: 53.7 us -> 53.8 us (level)
  no operation moved by 1% of the time
where the time goes in v5:
time: 53.8 us; the launch traced here: 53.6 us
  Pallas kernels  50.8 us (94%)
  local copies, waits for them, and re-layouts  2.17 us (4%)
  between operations  0.64 us (1%)
    pallas_call x1, Pallas kernels, on_device(): pl.pallas_call(body, out_shape=[jax.ShapeDtypeStruct((ROWS, HID, COLS), B...  50.8 us
    unnamed x2, local copies, waits for them, and re-layouts  2.17 us

profile of v5, /device:TPU:1, one launch (start us, length us, event | category | flops | bytes accessed | tf_op | source)
XLA Modules:
  0.0 53.6 jit_solution(8119812998965833311)
XLA Ops:
  0.6 50.8 %reproject_and_step.1 = (bf16[32,32,256]{2,1,0:T(8,128)(2,1)S(1)}, bf16[32,32,256]{2,1,0:T(8,128)(2,1)S(1)}) custom-call(s32[1,4,128]{2,1,0:T(4,128)} %bitcast.13, bf16[128,16,128]{2,1,0:T(8,128)(2,1)} %x_hbm.1, bf16[128,4,8,128]{3,2,1,0:T(8,128)(2,1)} %bitcast.10, bf16[32,32,256]{2,1,0:T(8,128)(2,1)} %hid_hbm.1, bf16[32,32,256]{2,1,0:T(8,128)(2,1)} %cell_hbm.1, ...), custom_call_target="tpu_custom_call" | custom-call | tf_op jit(solution)/shard_map/reproject_and_step/pallas_call | solution.py:496
  51.5 1.1 %copy.12 = bf16[32,32,256]{2,1,0:T(8,128)(2,1)} copy(bf16[32,32,256]{2,0,1:T(8,128)(2,1)S(1)} %bitcast.9) | data formatting | bytes 1048576
  52.5 1.1 %copy.13 = bf16[32,32,256]{2,1,0:T(8,128)(2,1)} copy(bf16[32,32,256]{2,0,1:T(8,128)(2,1)S(1)} %bitcast.8) | data formatting | bytes 1048576

commit v6 on v4

--- a/solution.py
+++ b/solution.py
@@ -92,11 +92,11 @@
 
 
 def spread(halves, into, count, at):
-    row = jnp.concatenate(halves, axis=1)
+    row = jnp.concatenate(halves, axis=1).astype(BF16)
     where = pl.ds(at, COLS)
-    into[0:count, where] = roll(row, 1).astype(BF16)
-    into[count : 2 * count, where] = row.astype(BF16)
-    into[2 * count : 3 * count, where] = roll(row, COLS - 1).astype(BF16)
+    into[0:count, where] = roll(row, 1)
+    into[count : 2 * count, where] = row
+    into[2 * count : 3 * count, where] = roll(row, COLS - 1)
 
 
 def padded_at(y):
@@ -376,11 +376,16 @@
     fedge = fnear = jnp.zeros((CH, 128), F32)
     for y in range(ROWS):
         halves = cell_row(y)
-        spread(halves, fshifted, CH, padded_at(y))
         fedge = fouter.insert(fedge, y, halves)
         fnear = finner.insert(fnear, y, halves)
     stage(qf, cell_row, HALO, (fedge, fnear))
     swap(DEEP, qf, rf, near_send.at[STEPS], near_recv.at[STEPS])
+
+    def spread_cells(y, carry):
+        spread(cell_row(y), fshifted, CH, padded_at(y))
+        return carry
+
+    lax.fori_loop(0, ROWS, spread_cells, 0, unroll=4)
 
     fmini = None
     for t in range(STEPS):
@@ -399,11 +404,13 @@
                 hidden = jnp.where(in_globe(y), hidden, 0.0) if isinstance(y, int) else hidden
             halves = halves_of(hidden)
             for half, v in enumerate(halves_of(memory)):
-                cells[half, pl.ds(pl.multiple_of((y + 2) * HID, HID), HID)] = v
-            if last:
-                for half, v in enumerate(halves):
-                    rows[half, pl.ds(pl.multiple_of(y * HID, HID), HID)] = v
-            else:
+                if last:
+                    part = slice(half * 128, half * 128 + 128)
+                    hout_ref[y, :, part] = halves[half].astype(BF16)
+                    cout_ref[y, :, part] = v.astype(BF16)
+                else:
+                    cells[half, pl.ds(pl.multiple_of((y + 2) * HID, HID), HID)] = v
+            if not last:
                 spread(halves, there, HID, padded_at(y))
             return halves
 
@@ -425,22 +432,22 @@
         state = lax.fori_loop(0, (ROWS - 2) // (2 * BLOCK), inside, state)
 
         if t == 0:
-            for k, got in ((0, rh), (STEPS + 1, rc), (STEPS, rf)):
+            for k, got in ((0, rh), (STEPS + 1, rc)):
                 whole(got, near_send.at[k], near_recv.at[k]).wait_recv()
             halo_rows(rh, here, HID)
-            halo_rows(rf, fshifted, CH)
             for slot, y in ((1, -2), (3, -1), (5, 32), (7, 33)):
                 for half in range(2):
                     cells[half, (y + 2) * HID : (y + 3) * HID] = rc[slot + half].astype(F32)
             edge_cell = frame(HID, edge_cell, rc[0].astype(F32), rc[9].astype(F32))
+            mini = deep_taps(edge, near, rh, HID)
+            whole(rf, near_send.at[STEPS], near_recv.at[STEPS]).wait_recv()
+            halo_rows(rf, fshifted, CH)
             fmini = deep_taps(fedge, fnear, rf, CH)
         depth = STEPS - t
         low, high = gates_of(1 - depth, depth), gates_of(ROWS - 1, depth)
         above = [finish_row(-r, low[:, (depth - 1 - r) * COLS : (depth - r) * COLS]) for r in range(depth)]
         below = [finish_row(ROWS - 1 + r, high[:, r * COLS : (r + 1) * COLS]) for r in range(depth)]
-        if t == 0:
-            mini = deep_taps(edge, near, rh, HID)
-        else:
+        if t > 0:
             whole(re.at[t - 1], near_send.at[t], near_recv.at[t]).wait_recv()
             half = lanes((HID, 128)) < 64
             sides = roll(jnp.where(half, re[t - 1, 1].astype(F32), re[t - 1, 0].astype(F32)), 64)
@@ -472,11 +479,13 @@
                 part = there.at[block_at * HID : block_at * HID + HID, where]
                 part[...] = jnp.where(lane == spot, value, part[...])
 
-    for source, skip, columns, to in ((rows, 0, edge, hout_ref), (cells, 2, edge_cell, cout_ref)):
+    lane = lanes((HID, 128))
+    for columns, to in ((edge, hout_ref), (edge_cell, cout_ref)):
         for y in range(ROWS):
-            one, two = corners(columns, y, row_at(source, y + skip, HID))
-            to[y, :, :128] = one.astype(BF16)
-            to[y, :, 128:] = two.astype(BF16)
+            left = roll(columns, (-(y + HALO)) % 128).astype(BF16)
+            right = roll(columns, (63 - HALO - y) % 128).astype(BF16)
+            to[y, :, :128] = jnp.where(lane == 0, left, to[y, :, :128])
+            to[y, :, 128:] = jnp.where(lane == 127, right, to[y, :, 128:])
 
     sent = out_buf.at[pl.ds(1, PEERS - 1)]
     pltpu.make_async_remote_copy(

time: 53.7 us -> 53.6 us (level); the launches traced: 53.6 us -> 52.9 us
  Pallas kernels: 50.8 us -> 50.1 us
    pallas_call x1, Pallas kernels: 50.8 us -> 50.1 us  [on_device(): pl.pallas_call(body, out_shape=[jax.ShapeDtypeStruct((ROWS, HID, COLS), B...]
where the time goes in v6:
time: 53.6 us; the launch traced here: 52.9 us
  Pallas kernels  50.1 us (93%)
  local copies, waits for them, and re-layouts  2.17 us (4%)
  between operations  0.64 us (1%)
    pallas_call x1, Pallas kernels, on_device(): pl.pallas_call(body, out_shape=[jax.ShapeDtypeStruct((ROWS, HID, COLS), B...  50.1 us
    unnamed x2, local copies, waits for them, and re-layouts  2.17 us

profile of v6, /device:TPU:1, one launch (start us, length us, event | category | flops | bytes accessed | tf_op | source)
XLA Modules:
  0.0 52.9 jit_solution(36476217875871778)
XLA Ops:
  0.6 50.1 %reproject_and_step.1 = (bf16[32,32,256]{2,1,0:T(8,128)(2,1)S(1)}, bf16[32,32,256]{2,1,0:T(8,128)(2,1)S(1)}) custom-call(s32[1,4,128]{2,1,0:T(4,128)} %bitcast.13, bf16[128,16,128]{2,1,0:T(8,128)(2,1)} %x_hbm.1, bf16[128,4,8,128]{3,2,1,0:T(8,128)(2,1)} %bitcast.10, bf16[32,32,256]{2,1,0:T(8,128)(2,1)} %hid_hbm.1, bf16[32,32,256]{2,1,0:T(8,128)(2,1)} %cell_hbm.1, ...), custom_call_target="tpu_custom_call" | custom-call | tf_op jit(solution)/shard_map/reproject_and_step/pallas_call | solution.py:514
  50.8 1.1 %copy.12 = bf16[32,32,256]{2,1,0:T(8,128)(2,1)} copy(bf16[32,32,256]{2,0,1:T(8,128)(2,1)S(1)} %bitcast.9) | data formatting | bytes 1048576
  51.8 1.1 %copy.13 = bf16[32,32,256]{2,1,0:T(8,128)(2,1)} copy(bf16[32,32,256]{2,0,1:T(8,128)(2,1)S(1)} %bitcast.8) | data formatting | bytes 1048576

commit v7 on v6

--- a/solution.py
+++ b/solution.py
@@ -444,9 +444,6 @@
             halo_rows(rf, fshifted, CH)
             fmini = deep_taps(fedge, fnear, rf, CH)
         depth = STEPS - t
-        low, high = gates_of(1 - depth, depth), gates_of(ROWS - 1, depth)
-        above = [finish_row(-r, low[:, (depth - 1 - r) * COLS : (depth - r) * COLS]) for r in range(depth)]
-        below = [finish_row(ROWS - 1 + r, high[:, r * COLS : (r + 1) * COLS]) for r in range(depth)]
         if t > 0:
             whole(re.at[t - 1], near_send.at[t], near_recv.at[t]).wait_recv()
             half = lanes((HID, 128)) < 64
@@ -456,19 +453,25 @@
         gates = jnp.dot(weight[:, :448], mini, preferred_element_type=F32)
         edge, edge_cell = update(gates, edge_cell)
         if last:
+            low, high = gates_of(1 - depth, depth), gates_of(ROWS - 1, depth)
+            above = [finish_row(-r, low[:, (depth - 1 - r) * COLS : (depth - r) * COLS]) for r in range(depth)]
+            below = [finish_row(ROWS - 1 + r, high[:, r * COLS : (r + 1) * COLS]) for r in range(depth)]
             break
         lane = lanes((HID, 128))
         edge = jnp.where(in_globe(jnp.where(lane < 64, lane, lane - 64) - HALO), edge, 0.0)
         qe[t, 0] = edge.astype(BF16)
+        left = {y: roll(edge, (1 - HALO - y) % 128).astype(BF16) for y in range(1 - depth, ROWS + depth)}
+        right = {y: roll(edge, (63 - HALO - y) % 128).astype(BF16) for y in range(1 - depth, ROWS + depth)}
+        swap(SIDES, qe.at[t], re.at[t], near_send.at[t + 1], near_recv.at[t + 1])
+        low, high = gates_of(1 - depth, depth), gates_of(ROWS - 1, depth)
+        above = [finish_row(-r, low[:, (depth - 1 - r) * COLS : (depth - r) * COLS]) for r in range(depth)]
+        below = [finish_row(ROWS - 1 + r, high[:, r * COLS : (r + 1) * COLS]) for r in range(depth)]
         for halves in above:
             state = inner.take(state, halves)
         near = inner.place(state, 1 - depth)
         near = jnp.where((lane == 34) | (lane == 98), 0.0, near)
         for r, halves in enumerate(below):
             near = inner.insert(near, ROWS - 1 + r, halves)
-        left = {y: roll(edge, (1 - HALO - y) % 128).astype(BF16) for y in range(1 - depth, ROWS + depth)}
-        right = {y: roll(edge, (63 - HALO - y) % 128).astype(BF16) for y in range(1 - depth, ROWS + depth)}
-        swap(SIDES, qe.at[t], re.at[t], near_send.at[t + 1], near_recv.at[t + 1])
         for y in range(1 - depth, ROWS + depth - 1):
             first = pl.ds(padded_at(y), 128)
             second = pl.ds(padded_at(y) + 128, 128)

time: 53.6 us -> 53.5 us (level)
  no operation moved by 1% of the time
where the time goes in v7:
time: 53.5 us; the launch traced here: 52.7 us
  Pallas kernels  49.9 us (93%)
  local copies, waits for them, and re-layouts  2.17 us (4%)
  between operations  0.64 us (1%)
    pallas_call x1, Pallas kernels, on_device(): pl.pallas_call(body, out_shape=[jax.ShapeDtypeStruct((ROWS, HID, COLS), B...  49.9 us
    unnamed x2, local copies, waits for them, and re-layouts  2.17 us

profile of v7, /device:TPU:1, one launch (start us, length us, event | category | flops | bytes accessed | tf_op | source)
XLA Modules:
  0.0 52.7 jit_solution(6380662306575562739)
XLA Ops:
  0.6 49.9 %reproject_and_step.1 = (bf16[32,32,256]{2,1,0:T(8,128)(2,1)S(1)}, bf16[32,32,256]{2,1,0:T(8,128)(2,1)S(1)}) custom-call(s32[1,4,128]{2,1,0:T(4,128)} %bitcast.13, bf16[128,16,128]{2,1,0:T(8,128)(2,1)} %x_hbm.1, bf16[128,4,8,128]{3,2,1,0:T(8,128)(2,1)} %bitcast.10, bf16[32,32,256]{2,1,0:T(8,128)(2,1)} %hid_hbm.1, bf16[32,32,256]{2,1,0:T(8,128)(2,1)} %cell_hbm.1, ...), custom_call_target="tpu_custom_call" | custom-call | tf_op jit(solution)/shard_map/reproject_and_step/pallas_call | solution.py:517
  50.5 1.1 %copy.12 = bf16[32,32,256]{2,1,0:T(8,128)(2,1)} copy(bf16[32,32,256]{2,0,1:T(8,128)(2,1)S(1)} %bitcast.9) | data formatting | bytes 1048576
  51.6 1.1 %copy.13 = bf16[32,32,256]{2,1,0:T(8,128)(2,1)} copy(bf16[32,32,256]{2,0,1:T(8,128)(2,1)S(1)} %bitcast.8) | data formatting | bytes 1048576
